TPU v7x, 512 devices: a whole 4x4x16 slice. The times are simulated.
512 devices in a mesh: cont: 16 (over x, y), net: 32 (over z, core).
Axes of the slice: x: 4, y: 4, z: 16, core: 2. Of those that a mesh axis runs over, the one named last changes fastest.
Arguments:
- angles: float32 [1024, 16384], P('cont', 'net'), may hold values from -6 to 6
- lam_from: float32 [1024, 20480], P('cont', 'net'), may hold values from -4 to 4
- lam_to: float32 [1024, 20480], P('cont', 'net'), may hold values from -4 to 4
- gen_dual: float32 [1024, 16384], P('cont', 'net'), may hold values from -6 to 6
- base_prev: float32 [16384], P('net'), may hold values from 0 to 0.5
- outage: int32 [1024, 20480], P('cont', 'net'), may hold values 0 or 1
- from_bus: int32 [20480], P('net'), may hold values from 0 to 511
- to_ref: int32 [20480], P('net'), may hold values from 0 to 639, as said below
- halo_rows: int32 [4096], P('net'), may hold values from 0 to 512, as said below
- stiffness: float32 [20480], P('net'), may hold values from 0.5 to 8
- bus_load: float32 [16384], P('net'), may hold values from -3 to 3
- gen_cost: float32 [16384], P('net'), may hold values from 0.25 to 4
- gen_limit: float32 [16384], P('net'), may hold values from 0.05 to 0.6
Outputs:
- angle_field: float32 [1024, 16384], P('cont', 'net')
- generation: float32 [1024, 16384], P('cont', 'net')
- base_setpoint: float32 [16384], P('net')
Inputs may be any that keep to these rules, and one draw needn't show every extreme that they name: `halo_rows`: in each partition's 128 entries the live rows come first and are distinct buses of that partition, the rest equal 512; the first partition has no live entry; some partition has all 128 entries live, the others at least half. `to_ref`: A value below 512 is a bus of the branch's own partition; 512 + s names live slot s of the next partition's list; branches of the last partition are all local.
All inputs are finite; a program needn't handle non-finite values. No bound on the sum of `outage` on one device may be relied on, other than what follows from the above.
Results may differ from a plain program's by a relative error of at most 0.0001.
Values sent between devices are 32-bit elements; how exact they have to be, the bound alone decides.
A program may use at most 64 MiB of HBM per device.

v0:
```python
import jax
import jax.numpy as jnp
from jax import lax
from jax.sharding import PartitionSpec as P

ROUNDS = 4


penalty = 1.0
balance = 2.0


def from_behind(value, axis, by):
    peers = lax.axis_size(axis)
    pairs = [(i, i + by) for i in range(peers) if 0 <= i + by < peers]
    return lax.ppermute(value, axis, pairs)


def copy_for_each(value, axis):
    peers = lax.axis_size(axis)
    return lax.all_to_all(
        jnp.broadcast_to(value[None], (peers, *value.shape)), axis, 0, 0, tiled=True
    )


def taken_together(value, axis):
    everything = copy_for_each(value, axis)
    return jnp.sum(everything, axis=0)


def one_hot_rows(index, count):
    return (index[:, None] == jnp.arange(count, dtype=jnp.int32)[None, :]).astype(jnp.float32)


def lookup(values, table):
    return lax.dot_general(
        values,
        table,
        (((1,), (1,)), ((), ())),
        precision=lax.Precision.HIGHEST,
        preferred_element_type=jnp.float32,
    )


def spread(values, table):
    return jnp.dot(
        values, table, precision=lax.Precision.HIGHEST, preferred_element_type=jnp.float32
    )


def branch_step(theta_from, theta_to, lam_f, lam_t, copy_f, copy_t, weights, later):
    if later:
        lam_f = lam_f + penalty * (copy_f - theta_from)
        lam_t = lam_t + penalty * (copy_t - theta_to)
    target_from = theta_from - lam_f / penalty
    target_to = theta_to - lam_t / penalty
    angle_gap = penalty * (target_from - target_to) / (penalty + 2.0 * weights)
    centre = 0.5 * (target_from + target_to)
    copy_f = centre + 0.5 * angle_gap
    copy_t = centre - 0.5 * angle_gap
    return (lam_f, lam_t, copy_f, copy_t, weights * angle_gap)


def local(
    angles,
    lam_from,
    lam_to,
    gen_dual,
    base_prev,
    outage,
    from_bus,
    to_ref,
    halo_rows,
    stiffness,
    bus_load,
    gen_cost,
    gen_limit,
):
    local_count = angles.shape[1]
    cont_local = angles.shape[0]
    slot_count = halo_rows.shape[0]
    branch_count = from_bus.shape[0]
    contingencies = cont_local * lax.axis_size("cont")
    weighted = stiffness[None, :] * (1.0 - outage.astype(jnp.float32))
    extended = local_count + slot_count
    branch_table = jnp.concatenate(
        [one_hot_rows(from_bus, extended), one_hot_rows(to_ref, extended)], axis=0
    )
    count_ext = jnp.sum(branch_table, axis=0)
    own_table = one_hot_rows(halo_rows, local_count)
    theta = angles
    base_set = base_prev
    copy_from = jnp.zeros_like(lam_from)
    copy_to = jnp.zeros_like(lam_to)
    generation = jnp.zeros_like(gen_dual)
    for round_index in range(ROUNDS):
        picked = lookup(theta, own_table)
        theta_ext = jnp.concatenate([theta, from_behind(picked, "net", -1)], axis=1)
        ends = lookup(theta_ext, branch_table)
        theta_from = ends[:, :branch_count]
        theta_to = ends[:, branch_count:]
        lam_from, lam_to, copy_from, copy_to, branch_flow = branch_step(
            theta_from, theta_to, lam_from, lam_to, copy_from, copy_to, weighted, round_index > 0
        )
        copy_terms = jnp.concatenate(
            [copy_from + lam_from / penalty, copy_to + lam_to / penalty], axis=1
        )
        flow_terms = jnp.concatenate([branch_flow, -branch_flow], axis=1)
        sums_ext = spread(jnp.concatenate([copy_terms, flow_terms], axis=0), branch_table)
        copy_ext = sums_ext[:cont_local]
        flow_ext = sums_ext[cont_local:]
        copy_in, flow_in, count_in = from_behind(
            (copy_ext[:, local_count:], flow_ext[:, local_count:], count_ext[local_count:]),
            "net",
            1,
        )
        stacked = spread(jnp.concatenate([copy_in, flow_in, count_in[None, :]], axis=0), own_table)
        copy_back = stacked[:cont_local]
        flow_back = stacked[cont_local : 2 * cont_local]
        count_back = stacked[2 * cont_local]
        copy_sum = copy_ext[:, :local_count] + copy_back
        net_out = flow_ext[:, :local_count] + flow_back
        degree = count_ext[:local_count] + count_back
        theta = copy_sum / (degree + 1.0)[None, :]
        generation = (
            penalty * base_set[None, :] - gen_dual + balance * (bus_load[None, :] + net_out)
        ) / (gen_cost + penalty + balance)[None, :]
        gen_dual = gen_dual + penalty * (generation - base_set[None, :])
        partial_value = jnp.sum(generation + gen_dual / penalty, axis=0)
        total = taken_together(partial_value, "cont")
        base_set = jnp.clip(total / contingencies, 0.0, gen_limit)
    return (theta, generation, base_set)


def solution(mesh):
    placed = (
        P("cont", "net"),
        P("cont", "net"),
        P("cont", "net"),
        P("cont", "net"),
        P("net"),
        P("cont", "net"),
        P("net"),
        P("net"),
        P("net"),
        P("net"),
        P("net"),
        P("net"),
        P("net"),
    )
    return jax.shard_map(
        local,
        mesh=mesh,
        in_specs=placed,
        out_specs=(P("cont", "net"), P("cont", "net"), P("net")),
        check_vma=False,
    )
```

profile of v0, /device:TPU:128, one launch (start us, length us, event | category | flops | bytes accessed | tf_op | source)
XLA Modules:
  0.0 138.7 jit_solution(3060406108694494843)
XLA Ops:
  1.8 1.9 %collective-permute-start.3 = (f32[128]{0:T(128)S(1)}, f32[128]{0:T(128)S(1)}, u32[]{:S(2)}, u32[]{:S(2)}) collective-permute-start(f32[128]{0:T(128)S(1)} %slice.149), channel_id=1, source_target_pairs={{0,1},{1,2},{2,3},{3,4},{4,5},{5,6},{6,7},{7,8},{8,9},{9,10},{10,1... | collective-permute-start | bytes 1544 | tf_op jit(solution)/shard_map/ppermute | solution.py:16
  5.0 5.0 %collective-permute-start = (f32[64,128]{1,0:T(8,128)S(1)}, f32[64,128]{1,0:T(8,128)S(1)}, u32[]{:S(2)}, u32[]{:S(2)}) collective-permute-start(f32[64,128]{1,0:T(8,128)S(1)} %convolution_bitcast_fusion), channel_id=1, source_target_pairs={{1,0},{2,1},{3,2},{4,3},{5,4},{6,5},{7,6},{8,7},{9,8},{10,9},{11,1... | collective-permute-start | bytes 98312 | tf_op jit(solution)/shard_map/ppermute | solution.py:16
  11.5 3.3 %fusion.43 = f32[64,1280]{1,0:T(8,128)S(1)} fusion(f32[64,128]{1,0:T(8,128)S(1)} %collective-permute-done, f32[64,512]{1,0:T(8,128)S(1)} %copy-done.34, f32[640,640]{1,0:T(8,128)S(1)} %get-tuple-element.50, f32[640,640]{1,0:T(8,128)S(1)} %get-tuple-element.49), kind=kOutput, calls=%fused_computation.50 | convolution fusion | flops 630005760 | bytes 3768320 | tf_op jit(solution)/shard_map/dot_general | solution.py:36
  15.8 2.2 %fusion.2 = f32[128,640]{1,0:T(8,128)S(1)} fusion(f32[64,640]{1,0:T(8,128)S(1)} %get-tuple-element.27, f32[64,640]{1,0:T(8,128)S(1)} %get-tuple-element.28, f32[64,640]{1,0:T(8,128)S(1)} %get-tuple-element.46, f32[64,640]{1,0:T(8,128)S(1)} %get-tuple-element.25, f32[640,640]{1,0:T(8,128)S(1)} %get-tuple-element.50, f32[640,640]{1,0:T(8,128)S(1)} %get-tuple-element.49), kind=kOutput, calls=%fused_computation.6 | convolution fusion | flops 1259601920 | bytes 4259840 | tf_op jit(solution)/shard_map/dot_general | solution.py:46
  17.9 2.7 %collective-permute-start.1 = (f32[64,128]{1,0:T(8,128)S(1)}, f32[64,128]{1,0:T(8,128)S(1)}, u32[]{:S(2)}, u32[]{:S(2)}) collective-permute-start(f32[64,128]{1,0:T(8,128)S(1)} %get-tuple-element.41), channel_id=1, source_target_pairs={{0,1},{1,2},{2,3},{3,4},{4,5},{5,6},{6,7},{7,8},{8,9},{9,10},{10,1... | collective-permute-start | bytes 98312 | tf_op jit(solution)/shard_map/ppermute | solution.py:16
  20.7 1.9 %collective-permute-start.2 = (f32[64,128]{1,0:T(8,128)S(1)}, f32[64,128]{1,0:T(8,128)S(1)}, u32[]{:S(2)}, u32[]{:S(2)}) collective-permute-start(f32[64,128]{1,0:T(8,128)S(1)} %get-tuple-element.42), channel_id=1, source_target_pairs={{0,1},{1,2},{2,3},{3,4},{4,5},{5,6},{6,7},{7,8},{8,9},{9,10},{10,1... | collective-permute-start | bytes 98312 | tf_op jit(solution)/shard_map/ppermute | solution.py:16
  24.4 2.7 %collective-permute-done.2 = f32[64,128]{1,0:T(8,128)S(1)} collective-permute-done((f32[64,128]{1,0:T(8,128)S(1)}, f32[64,128]{1,0:T(8,128)S(1)}, u32[]{:S(2)}, u32[]{:S(2)}) %collective-permute-start.2) | collective-permute-done | bytes 32800 | tf_op jit(solution)/shard_map/ppermute | solution.py:16
  31.8 14.5 %all_to_all.24 = f32[16,1,512]{2,1,0:T(1,128)S(1)} all-to-all(f32[16,1,512]{2,1,0:T(1,128)S(1)} %broadcast_in_dim.11), channel_id=1, replica_groups=mesh['cont'=16,'net'=32] {'cont'}, dimensions={0} | all-to-all | bytes 65536 | tf_op jit(solution)/shard_map/all_to_all | solution.py:21
  46.3 4.3 %fusion.47 = f32[64,1280]{1,0:T(8,128)S(1)} fusion(f32[64,128]{1,0:T(8,128)S(1)} %collective-permute-done.4, f32[64,512]{1,0:T(8,128)} %copy-done.32, f32[640,640]{1,0:T(8,128)S(1)} %get-tuple-element.50, f32[640,640]{1,0:T(8,128)S(1)} %get-tuple-element.49), kind=kOutput, calls=%fused_computation.54 | convolution fusion | flops 630005760 | bytes 3768320 | tf_op jit(solution)/shard_map/dot_general | solution.py:36
  51.6 2.1 %fusion.10 = f32[128,640]{1,0:T(8,128)S(1)} fusion(f32[64,640]{1,0:T(8,128)S(1)} %get-tuple-element.23, f32[64,640]{1,0:T(8,128)S(1)} %get-tuple-element.24, f32[64,640]{1,0:T(8,128)S(1)} %get-tuple-element.45, f32[64,640]{1,0:T(8,128)S(1)} %get-tuple-element.19, f32[640,640]{1,0:T(8,128)S(1)} %get-tuple-element.50, f32[640,640]{1,0:T(8,128)S(1)} %get-tuple-element.49), kind=kOutput, calls=%fused_computation.14 | convolution fusion | flops 1259601920 | bytes 4259840 | tf_op jit(solution)/shard_map/dot_general | solution.py:46
  53.8 1.9 %collective-permute-start.5 = (f32[64,128]{1,0:T(8,128)S(1)}, f32[64,128]{1,0:T(8,128)S(1)}, u32[]{:S(2)}, u32[]{:S(2)}) collective-permute-start(f32[64,128]{1,0:T(8,128)S(1)} %get-tuple-element.39), channel_id=1, source_target_pairs={{0,1},{1,2},{2,3},{3,4},{4,5},{5,6},{6,7},{7,8},{8,9},{9,10},{10,1... | collective-permute-start | bytes 98312 | tf_op jit(solution)/shard_map/ppermute | solution.py:16
  55.7 2.9 %collective-permute-start.6 = (f32[64,128]{1,0:T(8,128)S(1)}, f32[64,128]{1,0:T(8,128)S(1)}, u32[]{:S(2)}, u32[]{:S(2)}) collective-permute-start(f32[64,128]{1,0:T(8,128)S(1)} %get-tuple-element.40), channel_id=1, source_target_pairs={{0,1},{1,2},{2,3},{3,4},{4,5},{5,6},{6,7},{7,8},{8,9},{9,10},{10,1... | collective-permute-start | bytes 98312 | tf_op jit(solution)/shard_map/ppermute | solution.py:16
  60.2 2.1 %collective-permute-done.6 = f32[64,128]{1,0:T(8,128)S(1)} collective-permute-done((f32[64,128]{1,0:T(8,128)S(1)}, f32[64,128]{1,0:T(8,128)S(1)}, u32[]{:S(2)}, u32[]{:S(2)}) %collective-permute-start.6) | collective-permute-done | bytes 32800 | tf_op jit(solution)/shard_map/ppermute | solution.py:16
  68.0 10.7 %all_to_all.25 = f32[16,1,512]{2,1,0:T(1,128)S(1)} all-to-all(f32[16,1,512]{2,1,0:T(1,128)S(1)} %broadcast_in_dim.12), channel_id=1, replica_groups=mesh['cont'=16,'net'=32] {'cont'}, dimensions={0} | all-to-all | bytes 65536 | tf_op jit(solution)/shard_map/all_to_all | solution.py:21
  78.8 4.3 %fusion.51 = f32[64,1280]{1,0:T(8,128)S(1)} fusion(f32[64,128]{1,0:T(8,128)S(1)} %collective-permute-done.7, f32[64,512]{1,0:T(8,128)} %copy-done.31, f32[640,640]{1,0:T(8,128)S(1)} %get-tuple-element.50, f32[640,640]{1,0:T(8,128)S(1)} %get-tuple-element.49), kind=kOutput, calls=%fused_computation.58 | convolution fusion | flops 630005760 | bytes 3768320 | tf_op jit(solution)/shard_map/dot_general | solution.py:36
  84.1 2.2 %fusion.18 = f32[128,640]{1,0:T(8,128)S(1)} fusion(f32[64,640]{1,0:T(8,128)S(1)} %get-tuple-element.17, f32[64,640]{1,0:T(8,128)S(1)} %get-tuple-element.18, f32[64,640]{1,0:T(8,128)S(1)} %get-tuple-element.44, f32[64,640]{1,0:T(8,128)S(1)} %get-tuple-element.13, f32[640,640]{1,0:T(8,128)S(1)} %get-tuple-element.50, f32[640,640]{1,0:T(8,128)S(1)} %get-tuple-element.49), kind=kOutput, calls=%fused_computation.22 | convolution fusion | flops 1259601920 | bytes 4259840 | tf_op jit(solution)/shard_map/dot_general | solution.py:46
  90.1 2.6 %collective-permute-done.8 = f32[64,128]{1,0:T(8,128)S(1)} collective-permute-done((f32[64,128]{1,0:T(8,128)S(1)}, f32[64,128]{1,0:T(8,128)S(1)}, u32[]{:S(2)}, u32[]{:S(2)}) %collective-permute-start.8) | collective-permute-done | bytes 32800 | tf_op jit(solution)/shard_map/ppermute | solution.py:16
  92.7 1.9 %collective-permute-done.9 = f32[64,128]{1,0:T(8,128)S(1)} collective-permute-done((f32[64,128]{1,0:T(8,128)S(1)}, f32[64,128]{1,0:T(8,128)S(1)}, u32[]{:S(2)}, u32[]{:S(2)}) %collective-permute-start.9) | collective-permute-done | bytes 32800 | tf_op jit(solution)/shard_map/ppermute | solution.py:16
  99.3 10.7 %all_to_all.26 = f32[16,1,512]{2,1,0:T(1,128)S(1)} all-to-all(f32[16,1,512]{2,1,0:T(1,128)S(1)} %broadcast_in_dim.13), channel_id=1, replica_groups=mesh['cont'=16,'net'=32] {'cont'}, dimensions={0} | all-to-all | bytes 65536 | tf_op jit(solution)/shard_map/all_to_all | solution.py:21
  110.1 4.3 %fusion.55 = f32[64,1280]{1,0:T(8,128)S(1)} fusion(f32[64,128]{1,0:T(8,128)S(1)} %collective-permute-done.10, f32[64,512]{1,0:T(8,128)} %copy-done.33, f32[640,640]{1,0:T(8,128)S(1)} %get-tuple-element.50, f32[640,640]{1,0:T(8,128)S(1)} %get-tuple-element.49), kind=kOutput, calls=%fused_computation.62 | convolution fusion | flops 630005760 | bytes 3768320 | tf_op jit(solution)/shard_map/dot_general | solution.py:36
  114.6 2.2 %fusion.26 = f32[128,640]{1,0:T(8,128)S(1)} fusion(f32[64,640]{1,0:T(8,128)S(1)} %get-tuple-element.11, f32[64,640]{1,0:T(8,128)S(1)} %get-tuple-element.12, f32[64,640]{1,0:T(8,128)S(1)} %get-tuple-element.43, f32[64,640]{1,0:T(8,128)S(1)} %get-tuple-element.7, f32[640,640]{1,0:T(8,128)S(1)} %get-tuple-element.50, f32[640,640]{1,0:T(8,128)S(1)} %get-tuple-element.49), kind=kOutput, calls=%fused_computation.30 | convolution fusion | flops 1259601920 | bytes 4259840 | tf_op jit(solution)/shard_map/dot_general | solution.py:46
  120.7 2.6 %collective-permute-done.11 = f32[64,128]{1,0:T(8,128)S(1)} collective-permute-done((f32[64,128]{1,0:T(8,128)S(1)}, f32[64,128]{1,0:T(8,128)S(1)}, u32[]{:S(2)}, u32[]{:S(2)}) %collective-permute-start.11) | collective-permute-done | bytes 32800 | tf_op jit(solution)/shard_map/ppermute | solution.py:16
  123.2 1.9 %collective-permute-done.12 = f32[64,128]{1,0:T(8,128)S(1)} collective-permute-done((f32[64,128]{1,0:T(8,128)S(1)}, f32[64,128]{1,0:T(8,128)S(1)}, u32[]{:S(2)}, u32[]{:S(2)}) %collective-permute-start.12) | collective-permute-done | bytes 32800 | tf_op jit(solution)/shard_map/ppermute | solution.py:16
  127.4 10.7 %all_to_all.27 = f32[16,1,512]{2,1,0:T(1,128)S(1)} all-to-all(f32[16,1,512]{2,1,0:T(1,128)S(1)} %broadcast_in_dim.14), channel_id=1, replica_groups=mesh['cont'=16,'net'=32] {'cont'}, dimensions={0} | all-to-all | bytes 65536 | tf_op jit(solution)/shard_map/all_to_all | solution.py:21
  (149 shorter events, 35.7 us)
Async XLA Ops:
  1.8 20.9 %collective-permute-start.3 = (f32[128]{0:T(128)S(1)}, f32[128]{0:T(128)S(1)}, u32[]{:S(2)}, u32[]{:S(2)}) collective-permute-start(f32[128]{0:T(128)S(1)} %slice.149), channel_id=1, source_target_pairs={{0,1},{1,2},{2,3},{3,4},{4,5},{5,6},{6,7},{7,8},{8,9},{9,10},{10,1... | collective-permute-start | bytes 1544 | tf_op jit(solution)/shard_map/ppermute | solution.py:16
  5.0 6.6 %collective-permute-start = (f32[64,128]{1,0:T(8,128)S(1)}, f32[64,128]{1,0:T(8,128)S(1)}, u32[]{:S(2)}, u32[]{:S(2)}) collective-permute-start(f32[64,128]{1,0:T(8,128)S(1)} %convolution_bitcast_fusion), channel_id=1, source_target_pairs={{1,0},{2,1},{3,2},{4,3},{5,4},{6,5},{7,6},{8,7},{9,8},{10,9},{11,1... | collective-permute-start | bytes 98312 | tf_op jit(solution)/shard_map/ppermute | solution.py:16
  15.7 6.9 %copy-start.42 = (f32[512]{0:T(512)S(1)}, f32[512]{0:T(512)}, u32[]{:S(2)}) copy-start(f32[512]{0:T(512)} %param.24) | copy-start | bytes 6148
  15.7 11.4 %copy-start.39 = (s32[128]{0:T(128)S(1)}, s32[128]{0:T(128)}, u32[]{:S(2)}) copy-start(s32[128]{0:T(128)} %param.21) | copy-start | bytes 1540
  15.7 11.8 %copy-start.35 = (f32[64,512]{1,0:T(8,128)S(1)}, f32[64,512]{1,0:T(8,128)}, u32[]{:S(2)}) copy-start(f32[64,512]{1,0:T(8,128)} %param.16) | copy-start | bytes 393220
  15.7 11.8 %copy-start.38 = (f32[512]{0:T(512)S(1)}, f32[512]{0:T(512)}, u32[]{:S(2)}) copy-start(f32[512]{0:T(512)} %param.23) | copy-start | bytes 6148
  15.8 11.8 %copy-start.41 = (f32[512]{0:T(512)S(1)}, f32[512]{0:T(512)}, u32[]{:S(2)}) copy-start(f32[512]{0:T(512)} %param.17) | copy-start | bytes 6148
  17.9 9.6 %copy-start.8 = (f32[128,640]{1,0:T(8,128)}, f32[128,640]{1,0:T(8,128)S(1)}, u32[]{:S(2)}) copy-start(f32[128,640]{1,0:T(8,128)S(1)} %fusion.2) | copy-start | bytes 983044
  17.9 6.5 %collective-permute-start.1 = (f32[64,128]{1,0:T(8,128)S(1)}, f32[64,128]{1,0:T(8,128)S(1)}, u32[]{:S(2)}, u32[]{:S(2)}) collective-permute-start(f32[64,128]{1,0:T(8,128)S(1)} %get-tuple-element.41), channel_id=1, source_target_pairs={{0,1},{1,2},{2,3},{3,4},{4,5},{5,6},{6,7},{7,8},{8,9},{9,10},{10,1... | collective-permute-start | bytes 98312 | tf_op jit(solution)/shard_map/ppermute | solution.py:16
  20.7 6.4 %collective-permute-start.2 = (f32[64,128]{1,0:T(8,128)S(1)}, f32[64,128]{1,0:T(8,128)S(1)}, u32[]{:S(2)}, u32[]{:S(2)}) collective-permute-start(f32[64,128]{1,0:T(8,128)S(1)} %get-tuple-element.42), channel_id=1, source_target_pairs={{0,1},{1,2},{2,3},{3,4},{4,5},{5,6},{6,7},{7,8},{8,9},{9,10},{10,1... | collective-permute-start | bytes 98312 | tf_op jit(solution)/shard_map/ppermute | solution.py:16
  29.8 16.5 %collective-permute-start.4 = (f32[64,128]{1,0:T(8,128)}, f32[64,128]{1,0:T(8,128)S(1)}, u32[]{:S(2)}, u32[]{:S(2)}) collective-permute-start(f32[64,128]{1,0:T(8,128)} %fusion.41), channel_id=1, source_target_pairs={{1,0},{2,1},{3,2},{4,3},{5,4},{6,5},{7,6},{8,7},{9,8},{10,9},{11,1... | collective-permute-start | bytes 98312 | tf_op jit(solution)/shard_map/ppermute | solution.py:16
  51.6 7.0 %copy-start.40 = (f32[512]{0:T(512)S(1)}, f32[512]{0:T(512)}, u32[]{:S(2)}) copy-start(f32[512]{0:T(512)} %param.25) | copy-start | bytes 6148
  51.6 11.1 %copy-start.36 = (f32[64,512]{1,0:T(8,128)S(1)}, f32[64,512]{1,0:T(8,128)}, u32[]{:S(2)}) copy-start(f32[64,512]{1,0:T(8,128)} %param.16) | copy-start | bytes 393220
  53.8 6.4 %collective-permute-start.5 = (f32[64,128]{1,0:T(8,128)S(1)}, f32[64,128]{1,0:T(8,128)S(1)}, u32[]{:S(2)}, u32[]{:S(2)}) collective-permute-start(f32[64,128]{1,0:T(8,128)S(1)} %get-tuple-element.39), channel_id=1, source_target_pairs={{0,1},{1,2},{2,3},{3,4},{4,5},{5,6},{6,7},{7,8},{8,9},{9,10},{10,1... | collective-permute-start | bytes 98312 | tf_op jit(solution)/shard_map/ppermute | solution.py:16
  55.7 6.6 %collective-permute-start.6 = (f32[64,128]{1,0:T(8,128)S(1)}, f32[64,128]{1,0:T(8,128)S(1)}, u32[]{:S(2)}, u32[]{:S(2)}) collective-permute-start(f32[64,128]{1,0:T(8,128)S(1)} %get-tuple-element.40), channel_id=1, source_target_pairs={{0,1},{1,2},{2,3},{3,4},{4,5},{5,6},{6,7},{7,8},{8,9},{9,10},{10,1... | collective-permute-start | bytes 98312 | tf_op jit(solution)/shard_map/ppermute | solution.py:16
  66.1 12.7 %collective-permute-start.7 = (f32[64,128]{1,0:T(8,128)}, f32[64,128]{1,0:T(8,128)S(1)}, u32[]{:S(2)}, u32[]{:S(2)}) collective-permute-start(f32[64,128]{1,0:T(8,128)} %fusion.39), channel_id=1, source_target_pairs={{1,0},{2,1},{3,2},{4,3},{5,4},{6,5},{7,6},{8,7},{9,8},{10,9},{11,1... | collective-permute-start | bytes 98312 | tf_op jit(solution)/shard_map/ppermute | solution.py:16
  84.1 11.0 %copy-start.29 = (f32[64,512]{1,0:T(8,128)S(1)}, f32[64,512]{1,0:T(8,128)}, u32[]{:S(2)}) copy-start(f32[64,512]{1,0:T(8,128)} %get-tuple-element.6) | copy-start | bytes 393220
  86.2 8.8 %copy-start.7 = (f32[128,640]{1,0:T(8,128)}, f32[128,640]{1,0:T(8,128)S(1)}, u32[]{:S(2)}) copy-start(f32[128,640]{1,0:T(8,128)S(1)} %fusion.18) | copy-start | bytes 983044
  86.3 6.4 %collective-permute-start.8 = (f32[64,128]{1,0:T(8,128)S(1)}, f32[64,128]{1,0:T(8,128)S(1)}, u32[]{:S(2)}, u32[]{:S(2)}) collective-permute-start(f32[64,128]{1,0:T(8,128)S(1)} %get-tuple-element.37), channel_id=1, source_target_pairs={{0,1},{1,2},{2,3},{3,4},{4,5},{5,6},{6,7},{7,8},{8,9},{9,10},{10,1... | collective-permute-start | bytes 98312 | tf_op jit(solution)/shard_map/ppermute | solution.py:16
  88.2 6.4 %collective-permute-start.9 = (f32[64,128]{1,0:T(8,128)S(1)}, f32[64,128]{1,0:T(8,128)S(1)}, u32[]{:S(2)}, u32[]{:S(2)}) collective-permute-start(f32[64,128]{1,0:T(8,128)S(1)} %get-tuple-element.38), channel_id=1, source_target_pairs={{0,1},{1,2},{2,3},{3,4},{4,5},{5,6},{6,7},{7,8},{8,9},{9,10},{10,1... | collective-permute-start | bytes 98312 | tf_op jit(solution)/shard_map/ppermute | solution.py:16
  97.3 12.7 %collective-permute-start.10 = (f32[64,128]{1,0:T(8,128)}, f32[64,128]{1,0:T(8,128)S(1)}, u32[]{:S(2)}, u32[]{:S(2)}) collective-permute-start(f32[64,128]{1,0:T(8,128)} %fusion.37), channel_id=1, source_target_pairs={{1,0},{2,1},{3,2},{4,3},{5,4},{6,5},{7,6},{8,7},{9,8},{10,9},{11,1... | collective-permute-start | bytes 98312 | tf_op jit(solution)/shard_map/ppermute | solution.py:16
  114.6 10.9 %copy-start.30 = (f32[64,512]{1,0:T(8,128)S(1)}, f32[64,512]{1,0:T(8,128)}, u32[]{:S(2)}) copy-start(f32[64,512]{1,0:T(8,128)} %get-tuple-element.6) | copy-start | bytes 393220
  116.8 6.4 %collective-permute-start.11 = (f32[64,128]{1,0:T(8,128)S(1)}, f32[64,128]{1,0:T(8,128)S(1)}, u32[]{:S(2)}, u32[]{:S(2)}) collective-permute-start(f32[64,128]{1,0:T(8,128)S(1)} %get-tuple-element.35), channel_id=1, source_target_pairs={{0,1},{1,2},{2,3},{3,4},{4,5},{5,6},{6,7},{7,8},{8,9},{9,10},{10,1... | collective-permute-start | bytes 98312 | tf_op jit(solution)/shard_map/ppermute | solution.py:16
  118.7 6.4 %collective-permute-start.12 = (f32[64,128]{1,0:T(8,128)S(1)}, f32[64,128]{1,0:T(8,128)S(1)}, u32[]{:S(2)}, u32[]{:S(2)}) collective-permute-start(f32[64,128]{1,0:T(8,128)S(1)} %get-tuple-element.36), channel_id=1, source_target_pairs={{0,1},{1,2},{2,3},{3,4},{4,5},{5,6},{6,7},{7,8},{8,9},{9,10},{10,1... | collective-permute-start | bytes 98312 | tf_op jit(solution)/shard_map/ppermute | solution.py:16
  (32 other events, 82.3 us)
where the time goes:
time: 139 us
  blocking collectives  46.6 us (34%)
  matrix products  30.2 us (22%)
  starting transfers between devices  29.8 us (21%)
  waiting for transfers between devices  17.8 us (13%)
  other arithmetic  7.49 us (5%)
  local copies, waits for them, and re-layouts  5.31 us (4%)
  between operations  1.54 us (1%)
    all_to_all x4, blocking collectives, copy_for_each(): lax.all_to_all(jnp.broadcast_to(value[None], (peers, *value.shape)), axis...  46.6 us
    ppermute x13, starting transfers between devices, from_behind(): return lax.ppermute(value, axis, pairs)  29.8 us
    dot_general x8, matrix products, lookup(): lax.dot_general(values, table, (((1,), (1,)), ((), ())), precision=lax.Pr...  20.2 us
    ppermute x13, waiting for transfers between devices, from_behind(): return lax.ppermute(value, axis, pairs)  17.8 us
    dot_general x8, matrix products, spread(): jnp.dot(values, table, precision=lax.Precision.HIGHEST, preferred_element...  10 us
    unnamed x86, local copies, waits for them, and re-layouts  5.19 us
    reduce_sum x4, other arithmetic, local(): partial_value = jnp.sum(generation + gen_dual / penalty, axis=0)  3.7 us
  transfers between devices with their start and end apart: 13, of which 9 were waited for; matrix products, arithmetic and copies ran while one was open for 6% of the time, Pallas kernels for 0%

commit v1 on v0

v1 whole, which is shorter than its diff:
```python
import functools

import jax
import jax.numpy as jnp
from jax import lax
from jax.experimental import pallas as pl
from jax.experimental.pallas import tpu as pltpu
from jax.sharding import PartitionSpec as P

ROUNDS = 4
LANES = 128
penalty = 1.0
balance = 2.0
F32 = jnp.float32
BF16 = jnp.bfloat16
MESH = pl.DeviceIdType.MESH


def pieces(x):
    high = x.astype(BF16)
    low = (x - high.astype(F32)).astype(BF16)
    return jnp.concatenate([high, low], axis=0)


def fold(y):
    half = y.shape[0] // 2
    return y[:half] + y[half:]


def times(x2, table):
    return fold(jnp.dot(x2, table, preferred_element_type=F32))


def times_t(x2, table):
    return fold(
        lax.dot_general(x2, table, (((1,), (1,)), ((), ())), preferred_element_type=F32)
    )


def is_at(a, b):
    return jnp.where(a == b, 1.0, 0.0).astype(F32)


def kernel(
    n_cont,
    n_net,
    angles_h,
    lam_f_h,
    lam_t_h,
    dual_h,
    outage_h,
    from_h,
    to_h,
    rows_h,
    stiff_h,
    base_h,
    load_h,
    cost_h,
    limit_h,
    theta_o,
    gen_o,
    base_o,
    theta,
    lam_f,
    lam_t,
    dual,
    outage,
    from_v,
    to_v,
    rows_v,
    stiff,
    base_v,
    load,
    cost,
    limit,
    own,
    count,
    edge,
    edge_count,
    listed,
    first_left,
    first_right,
    in_right0,
    in_left0,
    out_left,
    out_right,
    in_left,
    in_right,
    c_out,
    c_in,
    theta_s,
    gen_s,
    base_s,
    in_sem,
    out_sem,
    first_send,
    first_recv,
    send_l,
    recv_l,
    send_r,
    recv_r,
    c_send,
    c_recv,
):
    conts, buses = theta.shape
    branches = lam_f.shape[1]
    slots = rows_v.shape[1]
    me = lax.axis_index("cont")
    part = lax.axis_index("net")
    has_left = part > 0
    has_right = part < n_net - 1

    loads = []
    for i, (src, dst) in enumerate(
        [
            (rows_h, rows_v),
            (from_h, from_v),
            (to_h, to_v),
            (angles_h, theta),
            (lam_f_h, lam_f),
            (lam_t_h, lam_t),
            (outage_h, outage),
            (stiff_h, stiff),
            (dual_h, dual),
            (base_h, base_v),
            (load_h, load),
            (cost_h, cost),
            (limit_h, limit),
        ]
    ):
        copy = pltpu.make_async_copy(src, dst, in_sem.at[i])
        copy.start()
        loads.append(copy)

    in_right0[...] = jnp.zeros_like(in_right0)
    in_left0[...] = jnp.zeros_like(in_left0)
    in_left[...] = jnp.zeros_like(in_left)
    in_right[...] = jnp.zeros_like(in_right)

    barrier = pltpu.get_barrier_semaphore()

    @pl.when(has_left)
    def _():
        pl.semaphore_signal(
            barrier, inc=1, device_id={"cont": me, "net": part - 1}, device_id_type=MESH
        )

    @pl.when(has_right)
    def _():
        pl.semaphore_signal(
            barrier, inc=1, device_id={"cont": me, "net": part + 1}, device_id_type=MESH
        )

    for j in range(1, n_cont):
        pl.semaphore_signal(
            barrier,
            inc=1,
            device_id={"cont": lax.rem(me + j, n_cont), "net": part},
            device_id_type=MESH,
        )

    for copy in loads[:3]:
        copy.wait()
    rows = rows_v[...]
    rows = jnp.where(rows < buses, rows, -1)
    rows_c = jnp.transpose(jnp.broadcast_to(rows.astype(F32), (slots, slots))).astype(jnp.int32)
    lane = lax.broadcasted_iota(jnp.int32, (slots, LANES), 1)
    slot_id = lax.broadcasted_iota(jnp.int32, (slots, LANES), 0)
    for j in range(buses // LANES):
        listed[:, j * LANES : (j + 1) * LANES] = is_at(rows_c, lane + j * LANES).astype(BF16)
    for j in range(branches // LANES):
        cols = slice(j * LANES, (j + 1) * LANES)
        start = from_v[j : j + 1, :]
        end = to_v[j : j + 1, :]
        a, b = is_at(rows_c, start), is_at(rows_c, end)
        edge[:slots, cols] = (a - b).astype(BF16)
        edge_count[:slots, cols] = (a + b).astype(BF16)
        c = is_at(slot_id + buses, end)
        edge[slots:, cols] = (-c).astype(BF16)
        edge_count[slots:, cols] = c.astype(BF16)

    ones = jnp.ones((16, branches), BF16)
    counts = lax.dot_general(
        ones, edge_count[...], (((1,), (1,)), ((), ())), preferred_element_type=F32
    )
    listed_count, slot_count = counts[:, :slots], counts[:, slots:]
    first_right[...] = slot_count
    first_left[conts:, :] = listed_count
    loads[3].wait()
    theta0 = theta[...]
    theta2 = pieces(theta0)
    first_left[:conts, :] = times_t(theta2, listed[...])

    def to_left(src, dst, s, r):
        return pltpu.make_async_remote_copy(
            src, dst, s, r, device_id={"cont": me, "net": part - 1}, device_id_type=MESH
        )

    def to_right(src, dst, s, r):
        return pltpu.make_async_remote_copy(
            src, dst, s, r, device_id={"cont": me, "net": part + 1}, device_id_type=MESH
        )

    first_l = to_left(first_left, in_right0, first_send.at[0], first_recv.at[0])
    first_r = to_right(first_right, in_left0, first_send.at[1], first_recv.at[1])

    inner = has_left & has_right

    @pl.when(inner)
    def _():
        pl.semaphore_wait(barrier, n_cont + 1)

    @pl.when(jnp.logical_not(inner))
    def _():
        pl.semaphore_wait(barrier, n_cont)

    @pl.when(has_left)
    def _():
        first_l.start()

    @pl.when(has_right)
    def _():
        first_r.start()

    bus_id = lax.broadcasted_iota(jnp.int32, (buses, LANES), 0)
    for j in range(branches // LANES):
        cols = slice(j * LANES, (j + 1) * LANES)
        a = is_at(bus_id, from_v[j : j + 1, :])
        b = is_at(bus_id, to_v[j : j + 1, :])
        own[:, cols] = (a - b).astype(BF16)
        count[:, cols] = (a + b).astype(BF16)
    delta = times(theta2, own[...])
    own_count = lax.dot_general(
        ones, count[...], (((1,), (1,)), ((), ())), preferred_element_type=F32
    )[:1]

    for copy in loads[4:]:
        copy.wait()
    share = []
    for j in range(branches // LANES):
        cols = slice(j * LANES, (j + 1) * LANES)
        full = stiff[j : j + 1, :]
        full = full / (penalty + 2.0 * full)
        share.append(full * (1.0 - outage[:, cols].astype(F32)))
    share = jnp.concatenate(share, axis=1)
    lam_gap = lam_f[...] - lam_t[...]

    inv_cost = 1.0 / (cost[...] + (penalty + balance))
    blocks = buses // LANES
    dual_part = dual[...]
    dual_sum = jnp.sum(dual_part, axis=0, keepdims=True)
    inv_row = jnp.concatenate([inv_cost[j : j + 1, :] for j in range(blocks)], axis=1)
    for j in range(blocks):
        c_out[0, blocks + j : blocks + j + 1, :] = dual_sum[:, j * LANES : (j + 1) * LANES]
    for r in range(1, ROUNDS):
        c_out[r, blocks:, :] = jnp.zeros((8 - blocks, LANES), F32)

    @pl.when(has_right)
    def _():
        first_l.wait_recv()

    @pl.when(has_left)
    def _():
        first_r.wait_recv()

    halo = in_right0[:conts, :]
    inv_halo = 1.0 / (in_right0[conts : conts + 1, :] + slot_count[:1] + 1.0)
    keep_halo = 1.0 - inv_halo
    left_count = in_left0[...]
    inv_listed = 1.0 / (listed_count[:1] + left_count[:1] + 1.0)
    degree = own_count + times(pieces(left_count), listed[...])[:1]
    inv_degree = 1.0 / (degree + 1.0)
    keep = 1.0 - inv_degree

    delta = delta + times(pieces(halo), edge[slots:, :])
    flow = share * (delta - lam_gap)
    now = theta0
    for r in range(ROUNDS):
        last = r == ROUNDS - 1
        flow2 = pieces(flow)
        sent = times_t(flow2, edge[...])
        slot_net = sent[:, slots:]
        out_right[r] = slot_net
        copy_r = to_right(out_right.at[r], in_left.at[r], send_r.at[r], recv_r.at[r])

        @pl.when(has_right)
        def _():
            copy_r.start()

        if not last:
            out_left[r] = sent[:, :slots]
            copy_l = to_left(out_left.at[r], in_right.at[r], send_l.at[r], recv_l.at[r])

            @pl.when(has_left)
            def _():
                copy_l.start()

        net = times_t(flow2, own[...])
        now = keep * now - net * inv_degree
        if not last:
            rest = 2.0 * times(pieces(now), own[...]) + (2.0 * flow - delta)

        @pl.when(has_left)
        def _():
            copy_r.wait_recv()

        if not last:

            @pl.when(has_right)
            def _():
                copy_l.wait_recv()

        left = in_left[r]
        if not last:
            halo = keep_halo * halo - (in_right[r] + slot_net) * inv_halo
            arrived = jnp.concatenate([-left * inv_listed, halo], axis=1)
            added = times(pieces(arrived), edge[...])
            gap = rest + 2.0 * added
            new_delta = 0.5 * (gap + delta) - flow
            flow = share * gap
            delta = new_delta

        spread = times(pieces(left), listed[...])
        net = net + spread
        now = now - spread * inv_degree
        if last:
            theta_s[...] = now
            pltpu.make_async_copy(theta_s, theta_o, out_sem.at[0]).start()
        net_sum = jnp.sum(net, axis=0, keepdims=True)
        for j in range(blocks):
            c_out[r, j : j + 1, :] = net_sum[:, j * LANES : (j + 1) * LANES]
        c_in[r, me] = c_out[r]
        for j in range(1, n_cont):
            pltpu.make_async_remote_copy(
                c_out.at[r],
                c_in.at[r, me],
                c_send.at[r],
                c_recv.at[r],
                device_id={"cont": lax.rem(me + j, n_cont), "net": part},
                device_id_type=MESH,
            ).start()
        if not last:
            dual_part = dual_part - (dual_part - 2.0 * net) * inv_row

    def arrived_sum(r):
        pltpu.make_async_copy(
            c_in.at[r, pl.ds(0, n_cont - 1)], c_in.at[r, pl.ds(0, n_cont - 1)], c_recv.at[r]
        ).wait()
        return jnp.sum(c_in[r], axis=0) * (1.0 / (n_cont * conts))

    x = base_v[...]
    loads_now = load[...]
    limits = limit[...]
    beta = jnp.zeros_like(x)
    mean_dual = None
    for r in range(ROUNDS):
        if r == ROUNDS - 1:
            row = (x - beta + balance * loads_now) * inv_cost
            part_gen = (balance * net - dual_part) * inv_row
            for j in range(blocks):
                cols = slice(j * LANES, (j + 1) * LANES)
                gen_s[:, cols] = part_gen[:, cols] + row[j : j + 1, :]
            pltpu.make_async_copy(gen_s, gen_o, out_sem.at[1]).start()
        mean = arrived_sum(r)
        if r == 0:
            mean_dual = mean[blocks:]
        mean_gen = (x - mean_dual + balance * (loads_now + mean[:blocks])) * inv_cost
        mean_dual = mean_dual + (mean_gen - x)
        beta = beta + (x + balance * loads_now - beta) * inv_cost - x
        x = jnp.clip(mean_gen + mean_dual, 0.0, limits)
    base_s[...] = x
    pltpu.make_async_copy(base_s, base_o, out_sem.at[2]).start()

    @pl.when(has_left)
    def _():
        first_l.wait_send()
        for r in range(ROUNDS - 1):
            to_left(out_left.at[r], in_right.at[r], send_l.at[r], recv_l.at[r]).wait_send()

    @pl.when(has_right)
    def _():
        first_r.wait_send()
        for r in range(ROUNDS):
            to_right(out_right.at[r], in_left.at[r], send_r.at[r], recv_r.at[r]).wait_send()

    for r in range(ROUNDS):
        pltpu.make_async_copy(
            c_in.at[r, pl.ds(0, n_cont - 1)], c_in.at[r, pl.ds(0, n_cont - 1)], c_send.at[r]
        ).wait()
    pltpu.make_async_copy(theta_s, theta_o, out_sem.at[0]).wait()
    pltpu.make_async_copy(gen_s, gen_o, out_sem.at[1]).wait()
    pltpu.make_async_copy(base_s, base_o, out_sem.at[2]).wait()


def local(
    n_cont,
    n_net,
    angles,
    lam_from,
    lam_to,
    gen_dual,
    base_prev,
    outage,
    from_bus,
    to_ref,
    halo_rows,
    stiffness,
    bus_load,
    gen_cost,
    gen_limit,
):
    conts, buses = angles.shape
    branches = from_bus.shape[0]
    slots = halo_rows.shape[0]
    blocks = buses // LANES

    def by_lanes(v):
        return v.reshape(v.shape[0] // LANES, LANES)

    anywhere = pl.BlockSpec(memory_space=pl.ANY)
    dma = pltpu.SemaphoreType.DMA
    vmem = pltpu.VMEM
    i32 = jnp.int32
    theta, generation, base = pl.pallas_call(
        functools.partial(kernel, n_cont, n_net),
        out_shape=(
            jax.ShapeDtypeStruct((conts, buses), F32),
            jax.ShapeDtypeStruct((conts, buses), F32),
            jax.ShapeDtypeStruct((blocks, LANES), F32),
        ),
        in_specs=[anywhere] * 13,
        out_specs=(anywhere,) * 3,
        scratch_shapes=[
            vmem((conts, buses), F32),
            vmem((conts, branches), F32),
            vmem((conts, branches), F32),
            vmem((conts, buses), F32),
            vmem((conts, branches), i32),
            vmem((branches // LANES, LANES), i32),
            vmem((branches // LANES, LANES), i32),
            vmem((1, slots), i32),
            vmem((branches // LANES, LANES), F32),
            vmem((blocks, LANES), F32),
            vmem((blocks, LANES), F32),
            vmem((blocks, LANES), F32),
            vmem((blocks, LANES), F32),
            vmem((buses, branches), BF16),
            vmem((buses, branches), BF16),
            vmem((2 * slots, branches), BF16),
            vmem((2 * slots, branches), BF16),
            vmem((slots, buses), BF16),
            vmem((conts + 16, slots), F32),
            vmem((16, slots), F32),
            vmem((conts + 16, slots), F32),
            vmem((16, slots), F32),
            vmem((ROUNDS, conts, slots), F32),
            vmem((ROUNDS, conts, slots), F32),
            vmem((ROUNDS, conts, slots), F32),
            vmem((ROUNDS, conts, slots), F32),
            vmem((ROUNDS, 8, LANES), F32),
            vmem((ROUNDS, n_cont, 8, LANES), F32),
            vmem((conts, buses), F32),
            vmem((conts, buses), F32),
            vmem((blocks, LANES), F32),
            dma((13,)),
            dma((3,)),
            dma((2,)),
            dma((2,)),
            dma((ROUNDS,)),
            dma((ROUNDS,)),
            dma((ROUNDS,)),
            dma((ROUNDS,)),
            dma((ROUNDS,)),
            dma((ROUNDS,)),
        ],
        compiler_params=pltpu.CompilerParams(collective_id=0, has_side_effects=True),
        name="rounds",
    )(
        angles,
        lam_from,
        lam_to,
        gen_dual,
        outage,
        by_lanes(from_bus),
        by_lanes(to_ref),
        by_lanes(halo_rows),
        by_lanes(stiffness),
        by_lanes(base_prev),
        by_lanes(bus_load),
        by_lanes(gen_cost),
        by_lanes(gen_limit),
    )
    return theta, generation, base.reshape(buses)


def solution(mesh):
    both = P("cont", "net")
    one = P("net")
    placed = (both, both, both, both, one, both, one, one, one, one, one, one, one)
    return jax.shard_map(
        functools.partial(local, mesh.shape["cont"], mesh.shape["net"]),
        mesh=mesh,
        in_specs=placed,
        out_specs=(both, both, one),
        check_vma=False,
    )
```

time: 139 us -> 32.9 us (0.24)
  the two profiles are of different devices: /device:TPU:128 before, /device:TPU:384 now
where the time goes in v1:
time: 32.9 us; the launch traced here: 32.7 us
  Pallas kernels  29.2 us (89%)
  local copies, waits for them, and re-layouts  2.86 us (9%)
  between operations  0.65 us (2%)
    pallas_call x1, Pallas kernels, local(): pl.pallas_call(functools.partial(kernel, n_cont, n_net), out_shape=(jax.S...  29.2 us
    unnamed x7, local copies, waits for them, and re-layouts  2.86 us

profile of v1, /device:TPU:384, one launch (start us, length us, event | category | flops | bytes accessed | tf_op | source)
XLA Modules:
  0.0 32.7 jit_solution(15401636091435061057)
XLA Ops:
  0.6 29.2 %rounds.1 = (f32[64,512]{1,0:T(8,128)}, f32[64,512]{1,0:T(8,128)}, f32[4,128]{1,0:T(4,128)}) custom-call(f32[64,512]{1,0:T(8,128)} %angles_h.1, f32[64,640]{1,0:T(8,128)} %lam_f_h.1, f32[64,640]{1,0:T(8,128)} %lam_t_h.1, f32[64,512]{1,0:T(8,128)} %dual_h.1, s32[64,640]{1,0:T(8,128)} %outage_h.1, s32[5,128]{1,0:T(8,128)} %bitcast.9, s32[5,128]{1,0:T(8,128)} %bitcast.10, ...), custom_call_target="tpu_custom_call" | custom-call | tf_op jit(solution)/shard_map/rounds/pallas_call | solution.py:424
  29.8 0.0 copy-start
  29.8 1.6 %copy.19 = f32[64,512]{1,0:T(8,128)} copy(f32[64,512]{1,0:T(8,128)} %get-tuple-element.12) | data formatting | bytes 262144
  31.4 0.0 copy-done
  31.4 0.0 copy-start.1
  31.4 0.7 %copy.20 = f32[64,512]{1,0:T(8,128)} copy(f32[64,512]{1,0:T(8,128)S(1)} %copy-done) | data formatting | bytes 262144
  32.1 0.0 copy-done.1
  32.1 0.6 %copy.21 = f32[512]{0:T(512)} copy(f32[512]{0:T(512)S(1)} %bitcast.16) | data formatting | bytes 4096
Async XLA Ops:
  29.8 1.6 %copy-start = (f32[64,512]{1,0:T(8,128)S(1)}, f32[64,512]{1,0:T(8,128)}, u32[]{:S(2)}) copy-start(f32[64,512]{1,0:T(8,128)} %get-tuple-element.13) | copy-start | bytes 393220
  31.4 0.7 %copy-start.1 = (f32[4,128]{1,0:T(4,128)S(1)}, f32[4,128]{1,0:T(4,128)}, u32[]{:S(2)}) copy-start(f32[4,128]{1,0:T(4,128)} %get-tuple-element.8) | copy-start | bytes 6148

commit v2 on v1

v2 whole, which is shorter than its diff:
```python
import functools

import jax
import jax.numpy as jnp
from jax import lax
from jax.experimental import pallas as pl
from jax.experimental.pallas import tpu as pltpu
from jax.sharding import PartitionSpec as P

ROUNDS = 4
LANES = 128
penalty = 1.0
balance = 2.0
F32 = jnp.float32
BF16 = jnp.bfloat16
MESH = pl.DeviceIdType.MESH


def pieces(x):
    high = x.astype(BF16)
    low = (x - high.astype(F32)).astype(BF16)
    return jnp.concatenate([high, low], axis=0)


def fold(y):
    half = y.shape[0] // 2
    return y[:half] + y[half:]


def times(x2, table):
    return fold(jnp.dot(x2, table, preferred_element_type=F32))


def times_t(x2, table):
    return fold(
        lax.dot_general(x2, table, (((1,), (1,)), ((), ())), preferred_element_type=F32)
    )


def times3(x, table):
    high = x.astype(BF16)
    rest = x - high.astype(F32)
    y = fold(jnp.dot(pieces(rest), table, preferred_element_type=F32))
    return y + jnp.dot(high, table, preferred_element_type=F32)


def is_at(a, b):
    return jnp.where(a == b, 1.0, 0.0).astype(F32)


def kernel(
    n_cont,
    n_net,
    row,
    angles_h,
    lam_f_h,
    lam_t_h,
    dual_h,
    outage_h,
    from_h,
    to_h,
    rows_h,
    stiff_h,
    base_h,
    load_h,
    cost_h,
    limit_h,
    theta_o,
    gen_o,
    base_o,
    theta,
    lam_f,
    lam_t,
    dual,
    outage,
    from_v,
    to_v,
    rows_v,
    stiff,
    base_v,
    load,
    cost,
    limit,
    own,
    count,
    edge,
    edge_count,
    listed,
    pick_out,
    pick_in,
    count_out,
    count_in,
    out_left,
    out_right,
    in_left,
    in_right,
    first_out,
    first_in,
    c_out,
    c_in,
    slot_out,
    slot_in,
    in_sem,
    pick_sem,
    count_send,
    count_recv,
    send_l,
    recv_l,
    send_r,
    recv_r,
    c_send,
    c_recv,
    slot_sem,
    plane_sem,
    next_sem,
):
    conts, buses = theta.shape
    branches = lam_f.shape[1]
    slots = rows_v.shape[1]
    blocks = buses // LANES
    me = lax.axis_index("cont")
    part = lax.axis_index("net")
    has_left = part > 0
    has_right = part < n_net - 1
    my_row, my_col = me // row, lax.rem(me, row)
    n_rows = n_cont // row

    def at(c, p):
        return dict(device_id={"cont": c, "net": p}, device_id_type=MESH)

    loads = []
    for i, (src, dst) in enumerate(
        [
            (rows_h, rows_v),
            (angles_h, theta),
            (from_h, from_v),
            (to_h, to_v),
            (lam_f_h, lam_f),
            (lam_t_h, lam_t),
            (outage_h, outage),
            (stiff_h, stiff),
            (dual_h, dual),
            (base_h, base_v),
            (load_h, load),
            (cost_h, cost),
            (limit_h, limit),
        ]
    ):
        copy = pltpu.make_async_copy(src, dst, in_sem.at[i])
        copy.start()
        loads.append(copy)

    @pl.when(jnp.logical_not(has_left))
    def _():
        count_in[0] = jnp.zeros((8, slots), F32)
        in_left[...] = jnp.zeros_like(in_left)
        slot_in[...] = jnp.zeros_like(slot_in)

    @pl.when(jnp.logical_not(has_right))
    def _():
        count_in[1] = jnp.zeros((8, slots), F32)
        pick_in[...] = jnp.zeros_like(pick_in)
        in_right[...] = jnp.zeros_like(in_right)

    barrier = pltpu.get_barrier_semaphore()
    column = [lax.rem(my_row + j, n_rows) * row + my_col for j in range(1, n_rows)]
    near = [my_row * row + lax.rem(my_col + j, row) for j in range(1, row)] + column

    @pl.when(has_left)
    def _():
        pl.semaphore_signal(barrier, inc=1, **at(me, part - 1))

    @pl.when(has_right)
    def _():
        pl.semaphore_signal(barrier, inc=1, **at(me, part + 1))

    for c in near:
        pl.semaphore_signal(barrier, inc=1, **at(c, part))

    loads[0].wait()
    rows = rows_v[...]
    rows = jnp.where(rows < buses, rows, -1)
    rows_c = jnp.transpose(jnp.broadcast_to(rows.astype(F32), (slots, slots))).astype(jnp.int32)
    lane = lax.broadcasted_iota(jnp.int32, (slots, LANES), 1)
    slot_id = lax.broadcasted_iota(jnp.int32, (slots, LANES), 0)
    for j in range(blocks):
        listed[:, j * LANES : (j + 1) * LANES] = is_at(rows_c, lane + j * LANES).astype(BF16)
    loads[1].wait()
    theta0 = theta[...]
    theta2 = pieces(theta0)
    pick_out[...] = times_t(theta2, listed[...])

    inner = has_left & has_right

    @pl.when(inner)
    def _():
        pl.semaphore_wait(barrier, len(near) + 2)

    @pl.when(jnp.logical_not(inner))
    def _():
        pl.semaphore_wait(barrier, len(near) + 1)

    def to_left(src, dst, s, r):
        return pltpu.make_async_remote_copy(src, dst, s, r, **at(me, part - 1))

    def to_right(src, dst, s, r):
        return pltpu.make_async_remote_copy(src, dst, s, r, **at(me, part + 1))

    pick = to_left(pick_out, pick_in, pick_sem.at[0], pick_sem.at[1])

    @pl.when(has_left)
    def _():
        pick.start()

    for c in column:
        pl.semaphore_signal(plane_sem, inc=1, **at(c, part))

    loads[2].wait()
    loads[3].wait()
    for j in range(branches // LANES):
        cols = slice(j * LANES, (j + 1) * LANES)
        start = from_v[j : j + 1, :]
        end = to_v[j : j + 1, :]
        a, b = is_at(rows_c, start), is_at(rows_c, end)
        edge[:slots, cols] = (a - b).astype(BF16)
        edge_count[:slots, cols] = (a + b).astype(BF16)
        c = is_at(slot_id + buses, end)
        edge[slots:, cols] = (-c).astype(BF16)
        edge_count[slots:, cols] = c.astype(BF16)

    ones = jnp.ones((16, branches), BF16)
    counts = lax.dot_general(
        ones, edge_count[...], (((1,), (1,)), ((), ())), preferred_element_type=F32
    )
    listed_count, slot_count = counts[:8, :slots], counts[:8, slots:]
    count_out[0] = listed_count
    count_out[1] = slot_count
    count_l = to_left(count_out.at[0], count_in.at[1], count_send.at[0], count_recv.at[0])
    count_r = to_right(count_out.at[1], count_in.at[0], count_send.at[1], count_recv.at[1])

    @pl.when(has_left)
    def _():
        count_l.start()

    @pl.when(has_right)
    def _():
        count_r.start()

    bus_id = lax.broadcasted_iota(jnp.int32, (buses, LANES), 0)
    for j in range(branches // LANES):
        cols = slice(j * LANES, (j + 1) * LANES)
        a = is_at(bus_id, from_v[j : j + 1, :])
        b = is_at(bus_id, to_v[j : j + 1, :])
        own[:, cols] = (a - b).astype(BF16)
        count[:, cols] = (a + b).astype(BF16)
    delta = times(theta2, own[...])

    for copy in loads[4:]:
        copy.wait()
    share = []
    for j in range(branches // LANES):
        cols = slice(j * LANES, (j + 1) * LANES)
        full = stiff[j : j + 1, :]
        full = full / (penalty + 2.0 * full)
        share.append(full * (1.0 - outage[:, cols].astype(F32)))
    share = jnp.concatenate(share, axis=1)
    lam_gap = lam_f[...] - lam_t[...]

    own_count = lax.dot_general(
        ones, count[...], (((1,), (1,)), ((), ())), preferred_element_type=F32
    )[:1]
    inv_cost = 1.0 / (cost[...] + (penalty + balance))
    dual_part = dual[...]
    dual_sum = jnp.sum(dual_part, axis=0, keepdims=True)
    inv_row = jnp.concatenate([inv_cost[j : j + 1, :] for j in range(blocks)], axis=1)
    for j in range(blocks):
        first_out[blocks + j : blocks + j + 1, :] = dual_sum[:, j * LANES : (j + 1) * LANES]

    @pl.when(has_right)
    def _():
        pick.wait_recv()

    halo = pick_in[...]
    delta = delta + times(pieces(halo), edge[slots:, :])
    flow = share * (delta - lam_gap)
    now = theta0
    net = net_here = None

    def share_sums(src, dst, s, r, sums):
        for j in range(blocks):
            src[j : j + 1, :] = sums[:, j * LANES : (j + 1) * LANES]
        dst[me] = src[...]
        for j in range(1, n_cont):
            pltpu.make_async_remote_copy(
                src, dst.at[me], s, r, **at(lax.rem(me + j, n_cont), part)
            ).start()

    for r in range(ROUNDS):
        last = r == ROUNDS - 1
        flow2 = pieces(flow)
        sent = times_t(flow2, edge[...])
        slot_net = sent[:, slots:]
        out_right[r] = slot_net
        copy_r = to_right(out_right.at[r], in_left.at[r], send_r.at[r], recv_r.at[r])

        @pl.when(has_right)
        def _():
            copy_r.start()

        if not last:
            out_left[r] = sent[:, :slots]
            copy_l = to_left(out_left.at[r], in_right.at[r], send_l.at[r], recv_l.at[r])

            @pl.when(has_left)
            def _():
                copy_l.start()

        net_here = times_t(flow2, own[...])
        if last:
            slot_out[...] = jnp.sum(slot_net, axis=0, keepdims=True)
            share_sums(
                c_out.at[r - 1],
                c_in.at[r - 1],
                c_send.at[r],
                c_recv.at[r],
                jnp.sum(net_here, axis=0, keepdims=True),
            )

            @pl.when(has_right)
            def _():
                pl.semaphore_wait(next_sem, 1)
                for j in range(n_cont):
                    pltpu.make_async_remote_copy(
                        slot_out,
                        slot_in.at[me],
                        slot_sem.at[0],
                        slot_sem.at[1],
                        **at(lax.rem(me + j, n_cont), part + 1),
                    ).start()

        if r == 0:

            @pl.when(has_right)
            def _():
                count_l.wait_recv()

            @pl.when(has_left)
            def _():
                count_r.wait_recv()

            left_count = count_in[0]
            inv_halo = 1.0 / (count_in[1][:1] + slot_count[:1] + 1.0)
            keep_halo = 1.0 - inv_halo
            inv_listed = 1.0 / (listed_count[:1] + left_count[:1] + 1.0)
            left_count = jnp.concatenate([left_count, left_count], axis=0)
            degree = own_count + times(pieces(left_count), listed[...])[:1]
            inv_degree = 1.0 / (degree + 1.0)
            keep = 1.0 - inv_degree
        else:
            spread = times(pieces(left), listed[...])
            net = net + spread
            now = now - spread * inv_degree
            if r == 1:
                pl.semaphore_wait(plane_sem, len(column))

                @pl.when(has_left)
                def _():
                    pl.semaphore_signal(next_sem, inc=1, **at(me, part - 1))

                share_sums(
                    first_out,
                    first_in,
                    c_send.at[0],
                    c_recv.at[0],
                    jnp.sum(net, axis=0, keepdims=True),
                )
            else:
                share_sums(
                    c_out.at[r - 2],
                    c_in.at[r - 2],
                    c_send.at[r - 1],
                    c_recv.at[r - 1],
                    jnp.sum(net, axis=0, keepdims=True),
                )
            dual_part = dual_part - (dual_part - 2.0 * net) * inv_row

        net = net_here
        now = keep * now - net * inv_degree
        if not last:
            rest = 2.0 * times(pieces(now), own[...]) + (2.0 * flow - delta)

        @pl.when(has_left)
        def _():
            copy_r.wait_recv()

        if not last:

            @pl.when(has_right)
            def _():
                copy_l.wait_recv()

        left = in_left[r]
        if not last:
            halo = keep_halo * halo - (in_right[r] + slot_net) * inv_halo
            arrived = jnp.concatenate([-left * inv_listed, halo], axis=1)
            added = times(pieces(arrived), edge[...])
            gap = rest + 2.0 * added
            delta, flow = 0.5 * (gap + delta) - flow, share * gap

    spread = times(pieces(left), listed[...])
    theta_o[...] = now - spread * inv_degree
    net = net + spread

    def taken(ref, sem):
        pltpu.make_async_copy(
            ref.at[pl.ds(0, n_cont - 1)], ref.at[pl.ds(0, n_cont - 1)], sem
        ).wait()

    x = base_v[...]
    loads_now = load[...]
    limits = limit[...]
    beta = jnp.zeros_like(x)
    scale = 1.0 / (n_cont * conts)
    mean_dual = None
    for r in range(ROUNDS):
        last = r == ROUNDS - 1
        if last:
            row_gen = (x - beta + balance * loads_now) * inv_cost
            part_gen = (balance * net - dual_part) * inv_row
            for j in range(blocks):
                cols = slice(j * LANES, (j + 1) * LANES)
                gen_o[:, cols] = part_gen[:, cols] + row_gen[j : j + 1, :]
        taken(first_in if r == 0 else c_in.at[r - 1], c_recv.at[r])
        total = jnp.sum(first_in[...] if r == 0 else c_in[r - 1], axis=0)
        if r == 0:
            mean_dual = total[blocks:] * scale
            total = total[:blocks]
        if last:

            @pl.when(has_left)
            def _():
                pltpu.make_async_copy(slot_in, slot_in, slot_sem.at[1]).wait()

            slot_sum = jnp.broadcast_to(jnp.sum(slot_in[...], axis=0), (16, slots))
            placed = times3(slot_sum, listed[...])
            total = total + jnp.concatenate(
                [placed[:1, j * LANES : (j + 1) * LANES] for j in range(blocks)], axis=0
            )
        mean = total * scale
        mean_gen = (x - mean_dual + balance * (loads_now + mean)) * inv_cost
        mean_dual = mean_dual + (mean_gen - x)
        beta = beta + (x + balance * loads_now - beta) * inv_cost - x
        x = jnp.clip(mean_gen + mean_dual, 0.0, limits)
    base_o[...] = x

    @pl.when(has_left)
    def _():
        pick.wait_send()
        count_l.wait_send()
        for r in range(ROUNDS - 1):
            to_left(out_left.at[r], in_right.at[r], send_l.at[r], recv_l.at[r]).wait_send()

    @pl.when(has_right)
    def _():
        count_r.wait_send()
        for r in range(ROUNDS):
            to_right(out_right.at[r], in_left.at[r], send_r.at[r], recv_r.at[r]).wait_send()
        pltpu.make_async_copy(slot_in, slot_in, slot_sem.at[0]).wait()

    for r in range(ROUNDS):
        taken(first_in if r == 0 else c_in.at[r - 1], c_send.at[r])


def finish(theta, gen, base, theta_o, gen_o, base_o, sem):
    copies = [
        pltpu.make_async_copy(src, dst, sem.at[i])
        for i, (src, dst) in enumerate([(theta, theta_o), (gen, gen_o), (base, base_o)])
    ]
    for copy in copies:
        copy.start()
    for copy in copies:
        copy.wait()


def local(
    n_cont,
    n_net,
    angles,
    lam_from,
    lam_to,
    gen_dual,
    base_prev,
    outage,
    from_bus,
    to_ref,
    halo_rows,
    stiffness,
    bus_load,
    gen_cost,
    gen_limit,
):
    conts, buses = angles.shape
    branches = from_bus.shape[0]
    slots = halo_rows.shape[0]
    blocks = buses // LANES
    row = n_cont
    for r in range(1, n_cont + 1):
        if n_cont % r == 0 and r * r <= n_cont:
            row = r

    def by_lanes(v):
        return v.reshape(v.shape[0] // LANES, LANES)

    inside = pl.BlockSpec(memory_space=pltpu.VMEM)
    outside = pl.BlockSpec(memory_space=pltpu.HBM)
    dma = pltpu.SemaphoreType.DMA
    vmem = pltpu.VMEM
    i32 = jnp.int32
    kept = pl.pallas_call(
        functools.partial(kernel, n_cont, n_net, row),
        out_shape=(
            pltpu.VMEM((conts, buses), F32),
            pltpu.VMEM((conts, buses), F32),
            pltpu.VMEM((blocks, LANES), F32),
        ),
        in_specs=[outside] * 13,
        out_specs=(inside,) * 3,
        scratch_shapes=[
            vmem((conts, buses), F32),
            vmem((conts, branches), F32),
            vmem((conts, branches), F32),
            vmem((conts, buses), F32),
            vmem((conts, branches), i32),
            vmem((branches // LANES, LANES), i32),
            vmem((branches // LANES, LANES), i32),
            vmem((1, slots), i32),
            vmem((branches // LANES, LANES), F32),
            vmem((blocks, LANES), F32),
            vmem((blocks, LANES), F32),
            vmem((blocks, LANES), F32),
            vmem((blocks, LANES), F32),
            vmem((buses, branches), BF16),
            vmem((buses, branches), BF16),
            vmem((2 * slots, branches), BF16),
            vmem((2 * slots, branches), BF16),
            vmem((slots, buses), BF16),
            vmem((conts, slots), F32),
            vmem((conts, slots), F32),
            vmem((2, 8, slots), F32),
            vmem((2, 8, slots), F32),
            vmem((ROUNDS, conts, slots), F32),
            vmem((ROUNDS, conts, slots), F32),
            vmem((ROUNDS, conts, slots), F32),
            vmem((ROUNDS, conts, slots), F32),
            vmem((2 * blocks, LANES), F32),
            vmem((n_cont, 2 * blocks, LANES), F32),
            vmem((ROUNDS - 1, blocks, LANES), F32),
            vmem((ROUNDS - 1, n_cont, blocks, LANES), F32),
            vmem((1, slots), F32),
            vmem((n_cont, 1, slots), F32),
            dma((13,)),
            dma((2,)),
            dma((2,)),
            dma((2,)),
            dma((ROUNDS,)),
            dma((ROUNDS,)),
            dma((ROUNDS,)),
            dma((ROUNDS,)),
            dma((ROUNDS,)),
            dma((ROUNDS,)),
            dma((2,)),
            pltpu.SemaphoreType.REGULAR,
            pltpu.SemaphoreType.REGULAR,
        ],
        compiler_params=pltpu.CompilerParams(
            collective_id=0, has_side_effects=True
        ),
        name="rounds",
    )(
        angles,
        lam_from,
        lam_to,
        gen_dual,
        outage,
        by_lanes(from_bus),
        by_lanes(to_ref),
        by_lanes(halo_rows),
        by_lanes(stiffness),
        by_lanes(base_prev),
        by_lanes(bus_load),
        by_lanes(gen_cost),
        by_lanes(gen_limit),
    )
    theta, generation, base = pl.pallas_call(
        finish,
        out_shape=(
            jax.ShapeDtypeStruct((conts, buses), F32),
            jax.ShapeDtypeStruct((conts, buses), F32),
            jax.ShapeDtypeStruct((blocks, LANES), F32),
        ),
        in_specs=[inside] * 3,
        out_specs=(outside,) * 3,
        scratch_shapes=[dma((3,))],
        compiler_params=pltpu.CompilerParams(vmem_limit_bytes=4 << 20),
        name="finish",
    )(*kept)
    return theta, generation, base.reshape(buses)


def solution(mesh):
    both = P("cont", "net")
    one = P("net")
    placed = (both, both, both, both, one, both, one, one, one, one, one, one, one)
    return jax.shard_map(
        functools.partial(local, mesh.shape["cont"], mesh.shape["net"]),
        mesh=mesh,
        in_specs=placed,
        out_specs=(both, both, one),
        check_vma=False,
    )
```

time: 32.9 us -> 27 us (0.82)
  Pallas kernels: 29.2 us -> 26.2 us
  local copies, waits for them, and re-layouts: 2.86 us -> 0 us
    pallas_call x1 -> x2, Pallas kernels: 29.2 us -> 26.2 us  [the longest x1 25.5 us: local(): pl.pallas_call(functools.partial(kernel, n_cont, n_net, row), out_shape=(...]
    unnamed x7 -> x0, local copies, waits for them, and re-layouts: 2.86 us -> none
where the time goes in v2:
time: 27 us; the launch traced here: 26.9 us
  Pallas kernels  26.2 us (97%)
  between operations  0.64 us (2%)
    pallas_call x1, Pallas kernels, local(): pl.pallas_call(functools.partial(kernel, n_cont, n_net, row), out_shape=(...  25.5 us
    pallas_call x1, Pallas kernels, local(): pl.pallas_call(finish, out_shape=(jax.ShapeDtypeStruct((conts, buses), F3...  0.73 us

profile of v2, /device:TPU:384, one launch (start us, length us, event | category | flops | bytes accessed | tf_op | source)
XLA Modules:
  0.0 26.9 jit_solution(13081013891500045005)
XLA Ops:
  0.6 25.5 %rounds.1 = (f32[64,512]{1,0:T(8,128)S(1)}, f32[64,512]{1,0:T(8,128)S(1)}, f32[4,128]{1,0:T(4,128)S(1)}) custom-call(f32[64,512]{1,0:T(8,128)} %angles_h.1, f32[64,640]{1,0:T(8,128)} %lam_f_h.1, f32[64,640]{1,0:T(8,128)} %lam_t_h.1, f32[64,512]{1,0:T(8,128)} %dual_h.1, s32[64,640]{1,0:T(8,128)} %outage_h.1, s32[5,128]{1,0:T(8,128)} %bitcast.9, ...), custom_call_target="tpu_custom_call" | custom-call | tf_op jit(solution)/shard_map/rounds/pallas_call | solution.py:519
  26.1 0.7 %finish.1 = (f32[64,512]{1,0:T(8,128)}, f32[64,512]{1,0:T(8,128)}, f32[4,128]{1,0:T(4,128)}) custom-call(f32[64,512]{1,0:T(8,128)S(1)} %get-tuple-element.9.theta, f32[64,512]{1,0:T(8,128)S(1)} %get-tuple-element.10.gen, f32[4,128]{1,0:T(4,128)S(1)} %get-tuple-element.11.base), custom_call_target="tpu_custom_call" | custom-call | tf_op jit(solution)/shard_map/finish/pallas_call | solution.py:594

commit v3 on v2

--- a/solution.py
+++ b/solution.py
@@ -9,6 +9,8 @@
 
 ROUNDS = 4
 LANES = 128
+STREAMS = 2
+CHUNKS = 4
 penalty = 1.0
 balance = 2.0
 F32 = jnp.float32
@@ -35,13 +37,6 @@
     return fold(
         lax.dot_general(x2, table, (((1,), (1,)), ((), ())), preferred_element_type=F32)
     )
-
-
-def times3(x, table):
-    high = x.astype(BF16)
-    rest = x - high.astype(F32)
-    y = fold(jnp.dot(pieces(rest), table, preferred_element_type=F32))
-    return y + jnp.dot(high, table, preferred_element_type=F32)
 
 
 def is_at(a, b):
@@ -94,10 +89,12 @@
     out_right,
     in_left,
     in_right,
-    first_out,
-    first_in,
+    c0_out,
+    c0_in,
     c_out,
     c_in,
+    slot0_out,
+    slot0_in,
     slot_out,
     slot_in,
     in_sem,
@@ -108,8 +105,7 @@
     recv_l,
     send_r,
     recv_r,
-    c_send,
-    c_recv,
+    c_sem,
     slot_sem,
     plane_sem,
     next_sem,
@@ -118,11 +114,12 @@
     branches = lam_f.shape[1]
     slots = rows_v.shape[1]
     blocks = buses // LANES
+    part_rows = conts // STREAMS
     me = lax.axis_index("cont")
     part = lax.axis_index("net")
     has_left = part > 0
     has_right = part < n_net - 1
-    my_row, my_col = me // row, lax.rem(me, row)
+    my_row, my_col = lax.div(me, row), lax.rem(me, row)
     n_rows = n_cont // row
 
     def at(c, p):
@@ -154,6 +151,7 @@
     def _():
         count_in[0] = jnp.zeros((8, slots), F32)
         in_left[...] = jnp.zeros_like(in_left)
+        slot0_in[...] = jnp.zeros_like(slot0_in)
         slot_in[...] = jnp.zeros_like(slot_in)
 
     @pl.when(jnp.logical_not(has_right))
@@ -176,6 +174,14 @@
 
     for c in near:
         pl.semaphore_signal(barrier, inc=1, **at(c, part))
+
+    def hops(step):
+        return min(step[0], n_rows - step[0]) + min(step[1], row - step[1])
+
+    steps = sorted(((i, j) for i in range(n_rows) for j in range(row)), key=hops, reverse=True)
+    plane = [
+        lax.rem(my_row + i, n_rows) * row + lax.rem(my_col + j, row) for i, j in steps
+    ]
 
     loads[0].wait()
     rows = rows_v[...]
@@ -188,7 +194,9 @@
     loads[1].wait()
     theta0 = theta[...]
     theta2 = pieces(theta0)
-    pick_out[...] = times_t(theta2, listed[...])
+    picked = times_t(theta2, listed[...])
+    for s in range(STREAMS):
+        pick_out[s] = picked[s * part_rows : (s + 1) * part_rows]
 
     inner = has_left & has_right
 
@@ -206,11 +214,19 @@
     def to_right(src, dst, s, r):
         return pltpu.make_async_remote_copy(src, dst, s, r, **at(me, part + 1))
 
-    pick = to_left(pick_out, pick_in, pick_sem.at[0], pick_sem.at[1])
+    def pick(s):
+        return to_left(pick_out.at[s], pick_in.at[s], pick_sem.at[0, s], pick_sem.at[1, s])
+
+    def left_copy(r, s):
+        return to_left(out_left.at[r, s], in_right.at[r, s], send_l.at[r, s], recv_l.at[r, s])
+
+    def right_copy(r, s):
+        return to_right(out_right.at[r, s], in_left.at[r, s], send_r.at[r, s], recv_r.at[r, s])
 
     @pl.when(has_left)
     def _():
-        pick.start()
+        for s in range(STREAMS):
+            pick(s).start()
 
     for c in column:
         pl.semaphore_signal(plane_sem, inc=1, **at(c, part))
@@ -264,79 +280,100 @@
         full = full / (penalty + 2.0 * full)
         share.append(full * (1.0 - outage[:, cols].astype(F32)))
     share = jnp.concatenate(share, axis=1)
-    lam_gap = lam_f[...] - lam_t[...]
+    rest = delta - (lam_f[...] - lam_t[...])
 
     own_count = lax.dot_general(
         ones, count[...], (((1,), (1,)), ((), ())), preferred_element_type=F32
     )[:1]
     inv_cost = 1.0 / (cost[...] + (penalty + balance))
     dual_part = dual[...]
-    dual_sum = jnp.sum(dual_part, axis=0, keepdims=True)
     inv_row = jnp.concatenate([inv_cost[j : j + 1, :] for j in range(blocks)], axis=1)
-    for j in range(blocks):
-        first_out[blocks + j : blocks + j + 1, :] = dual_sum[:, j * LANES : (j + 1) * LANES]
-
-    @pl.when(has_right)
-    def _():
-        pick.wait_recv()
-
-    halo = pick_in[...]
-    delta = delta + times(pieces(halo), edge[slots:, :])
-    flow = share * (delta - lam_gap)
+
+    def store_sums(dst, values):
+        sums = jnp.sum(values, axis=0, keepdims=True)
+        for j in range(blocks):
+            dst[j : j + 1, :] = sums[:, j * LANES : (j + 1) * LANES]
+
+    store_sums(c0_out.at[2], dual_part)
+
+    def across(src, dst, sem):
+        dst[me] = src[...]
+        for c in plane[:-1]:
+            pltpu.make_async_remote_copy(
+                src, dst.at[me], sem.at[0], sem.at[1], **at(c, part)
+            ).start()
+
+    def onward(src, dst, sem):
+        @pl.when(has_right)
+        def _():
+            for c in plane:
+                pltpu.make_async_remote_copy(
+                    src, dst.at[me], sem.at[0], sem.at[1], **at(c, part + 1)
+                ).start()
+
+    halos = [None] * STREAMS
+    slot_nets = [None] * STREAMS
     now = theta0
-    net = net_here = None
-
-    def share_sums(src, dst, s, r, sums):
-        for j in range(blocks):
-            src[j : j + 1, :] = sums[:, j * LANES : (j + 1) * LANES]
-        dst[me] = src[...]
-        for j in range(1, n_cont):
-            pltpu.make_async_remote_copy(
-                src, dst.at[me], s, r, **at(lax.rem(me + j, n_cont), part)
-            ).start()
-
+    net = None
     for r in range(ROUNDS):
         last = r == ROUNDS - 1
-        flow2 = pieces(flow)
-        sent = times_t(flow2, edge[...])
-        slot_net = sent[:, slots:]
-        out_right[r] = slot_net
-        copy_r = to_right(out_right.at[r], in_left.at[r], send_r.at[r], recv_r.at[r])
-
-        @pl.when(has_right)
-        def _():
-            copy_r.start()
-
-        if not last:
-            out_left[r] = sent[:, :slots]
-            copy_l = to_left(out_left.at[r], in_right.at[r], send_l.at[r], recv_l.at[r])
-
-            @pl.when(has_left)
-            def _():
-                copy_l.start()
-
-        net_here = times_t(flow2, own[...])
-        if last:
-            slot_out[...] = jnp.sum(slot_net, axis=0, keepdims=True)
-            share_sums(
-                c_out.at[r - 1],
-                c_in.at[r - 1],
-                c_send.at[r],
-                c_recv.at[r],
-                jnp.sum(net_here, axis=0, keepdims=True),
-            )
+        lefts, flows, deltas = [], [], []
+        for s in range(STREAMS):
+            block = slice(s * part_rows, (s + 1) * part_rows)
 
             @pl.when(has_right)
             def _():
-                pl.semaphore_wait(next_sem, 1)
-                for j in range(n_cont):
-                    pltpu.make_async_remote_copy(
-                        slot_out,
-                        slot_in.at[me],
-                        slot_sem.at[0],
-                        slot_sem.at[1],
-                        **at(lax.rem(me + j, n_cont), part + 1),
-                    ).start()
+                if r == 0:
+                    pick(s).wait_recv()
+                else:
+                    left_copy(r - 1, s).wait_recv()
+
+            if r == 0:
+                halos[s] = pick_in[s]
+                added = times(pieces(halos[s]), edge[slots:, :])
+                deltas.append(delta[block] + added)
+                flows.append(share[block] * (rest[block] + added))
+            else:
+
+                @pl.when(has_left)
+                def _():
+                    right_copy(r - 1, s).wait_recv()
+
+                left = in_left[r - 1, s]
+                lefts.append(left)
+                halos[s] = keep_halo * halos[s] - (in_right[r - 1, s] + slot_nets[s]) * inv_halo
+                arrived = jnp.concatenate([-left * inv_listed, halos[s]], axis=1)
+                gap = rest[block] + 2.0 * times(pieces(arrived), edge[...])
+                deltas.append(0.5 * (gap + delta[block]) - flow[block])
+                flows.append(share[block] * gap)
+            sent = times_t(pieces(flows[s]), edge[...])
+            slot_nets[s] = sent[:, slots:]
+            out_right[r, s] = slot_nets[s]
+            if not last:
+                out_left[r, s] = sent[:, :slots]
+
+            @pl.when(has_right)
+            def _():
+                right_copy(r, s).start()
+
+            if not last:
+
+                @pl.when(has_left)
+                def _():
+                    left_copy(r, s).start()
+
+        flow = jnp.concatenate(flows, axis=0)
+        delta = jnp.concatenate(deltas, axis=0)
+        slot_sum = sum(jnp.sum(v, axis=0, keepdims=True) for v in slot_nets)
+        if r < 2:
+            slot0_out[r : r + 1, :] = slot_sum
+        else:
+            slot_out[r - 2] = slot_sum
+            onward(slot_out.at[r - 2], slot_in.at[r - 2], slot_sem.at[r - 1])
+        net_here = times_t(pieces(flow), own[...])
+        store_sums(c0_out.at[r] if r < 2 else c_out.at[r - 2], net_here)
+        if r >= 2:
+            across(c_out.at[r - 2], c_in.at[r - 2], c_sem.at[r - 1])
 
         if r == 0:
 
@@ -357,125 +394,125 @@
             inv_degree = 1.0 / (degree + 1.0)
             keep = 1.0 - inv_degree
         else:
-            spread = times(pieces(left), listed[...])
+            spread = times(pieces(jnp.concatenate(lefts, axis=0)), listed[...])
             net = net + spread
             now = now - spread * inv_degree
-            if r == 1:
-                pl.semaphore_wait(plane_sem, len(column))
-
-                @pl.when(has_left)
-                def _():
-                    pl.semaphore_signal(next_sem, inc=1, **at(me, part - 1))
-
-                share_sums(
-                    first_out,
-                    first_in,
-                    c_send.at[0],
-                    c_recv.at[0],
-                    jnp.sum(net, axis=0, keepdims=True),
-                )
-            else:
-                share_sums(
-                    c_out.at[r - 2],
-                    c_in.at[r - 2],
-                    c_send.at[r - 1],
-                    c_recv.at[r - 1],
-                    jnp.sum(net, axis=0, keepdims=True),
-                )
             dual_part = dual_part - (dual_part - 2.0 * net) * inv_row
 
         net = net_here
         now = keep * now - net * inv_degree
         if not last:
             rest = 2.0 * times(pieces(now), own[...]) + (2.0 * flow - delta)
-
+        if r == 0:
+            pl.semaphore_wait(plane_sem, len(column))
+
+            @pl.when(has_left)
+            def _():
+                pl.semaphore_signal(next_sem, inc=1, **at(me, part - 1))
+
+        if r == 1:
+
+            @pl.when(has_right)
+            def _():
+                pl.semaphore_wait(next_sem, 1)
+
+            onward(slot0_out, slot0_in, slot_sem.at[0])
+            across(c0_out, c0_in, c_sem.at[0])
+
+    def taken(ref, sem):
+        some = ref.at[pl.ds(0, n_cont - 1)]
+        pltpu.make_async_copy(some, some, sem).wait()
+
+    def taken_here(ref, sem):
         @pl.when(has_left)
         def _():
-            copy_r.wait_recv()
-
-        if not last:
-
-            @pl.when(has_right)
-            def _():
-                copy_l.wait_recv()
-
-        left = in_left[r]
-        if not last:
-            halo = keep_halo * halo - (in_right[r] + slot_net) * inv_halo
-            arrived = jnp.concatenate([-left * inv_listed, halo], axis=1)
-            added = times(pieces(arrived), edge[...])
-            gap = rest + 2.0 * added
-            delta, flow = 0.5 * (gap + delta) - flow, share * gap
-
-    spread = times(pieces(left), listed[...])
+            pltpu.make_async_copy(ref, ref, sem).wait()
+
+    def by_bus(slot_sums):
+        tall = jnp.concatenate(
+            [slot_sums, jnp.zeros((16 - slot_sums.shape[0], slots), F32)], axis=0
+        )
+        wide = times(pieces(tall), listed[...])
+        return [
+            jnp.concatenate([wide[r : r + 1, j * LANES : (j + 1) * LANES] for j in range(blocks)], axis=0)
+            for r in range(slot_sums.shape[0])
+        ]
+
+    loads_now = load[...]
+    limits = limit[...]
+    scale = 1.0 / (n_cont * conts)
+
+    def update(x, mean_dual, beta, total):
+        mean_gen = (x - mean_dual + balance * (loads_now + total * scale)) * inv_cost
+        mean_dual = mean_dual + (mean_gen - x)
+        beta = beta + (x + balance * loads_now - beta) * inv_cost - x
+        return jnp.clip(mean_gen + mean_dual, 0.0, limits), mean_dual, beta
+
+    taken(c0_in, c_sem.at[0, 1])
+    taken_here(slot0_in, slot_sem.at[0, 1])
+    total = jnp.sum(c0_in[...], axis=0)
+    moved = by_bus(jnp.sum(slot0_in[...], axis=0))
+    state = (base_v[...], total[2] * scale, jnp.zeros_like(loads_now))
+    for r in range(2):
+        state = update(*state, total[r] + moved[r])
+
+    lefts = []
+    for s in range(STREAMS):
+
+        @pl.when(has_left)
+        def _():
+            right_copy(ROUNDS - 1, s).wait_recv()
+
+        lefts.append(in_left[ROUNDS - 1, s])
+    spread = times(pieces(jnp.concatenate(lefts, axis=0)), listed[...])
     theta_o[...] = now - spread * inv_degree
     net = net + spread
-
-    def taken(ref, sem):
-        pltpu.make_async_copy(
-            ref.at[pl.ds(0, n_cont - 1)], ref.at[pl.ds(0, n_cont - 1)], sem
-        ).wait()
-
-    x = base_v[...]
-    loads_now = load[...]
-    limits = limit[...]
-    beta = jnp.zeros_like(x)
-    scale = 1.0 / (n_cont * conts)
-    mean_dual = None
-    for r in range(ROUNDS):
-        last = r == ROUNDS - 1
-        if last:
+    part_gen = (balance * net - dual_part) * inv_row
+
+    for r in range(2, ROUNDS):
+        if r == ROUNDS - 1:
+            x, _, beta = state
             row_gen = (x - beta + balance * loads_now) * inv_cost
-            part_gen = (balance * net - dual_part) * inv_row
             for j in range(blocks):
                 cols = slice(j * LANES, (j + 1) * LANES)
                 gen_o[:, cols] = part_gen[:, cols] + row_gen[j : j + 1, :]
-        taken(first_in if r == 0 else c_in.at[r - 1], c_recv.at[r])
-        total = jnp.sum(first_in[...] if r == 0 else c_in[r - 1], axis=0)
-        if r == 0:
-            mean_dual = total[blocks:] * scale
-            total = total[:blocks]
-        if last:
-
-            @pl.when(has_left)
-            def _():
-                pltpu.make_async_copy(slot_in, slot_in, slot_sem.at[1]).wait()
-
-            slot_sum = jnp.broadcast_to(jnp.sum(slot_in[...], axis=0), (16, slots))
-            placed = times3(slot_sum, listed[...])
-            total = total + jnp.concatenate(
-                [placed[:1, j * LANES : (j + 1) * LANES] for j in range(blocks)], axis=0
-            )
-        mean = total * scale
-        mean_gen = (x - mean_dual + balance * (loads_now + mean)) * inv_cost
-        mean_dual = mean_dual + (mean_gen - x)
-        beta = beta + (x + balance * loads_now - beta) * inv_cost - x
-        x = jnp.clip(mean_gen + mean_dual, 0.0, limits)
-    base_o[...] = x
+        taken(c_in.at[r - 2], c_sem.at[r - 1, 1])
+        taken_here(slot_in.at[r - 2], slot_sem.at[r - 1, 1])
+        total = jnp.sum(c_in[r - 2], axis=0)
+        moved = by_bus(jnp.sum(slot_in[r - 2], axis=0))
+        state = update(*state, total + moved[0])
+    base_o[...] = state[0]
 
     @pl.when(has_left)
     def _():
-        pick.wait_send()
+        for s in range(STREAMS):
+            pick(s).wait_send()
+            for r in range(ROUNDS - 1):
+                left_copy(r, s).wait_send()
         count_l.wait_send()
-        for r in range(ROUNDS - 1):
-            to_left(out_left.at[r], in_right.at[r], send_l.at[r], recv_l.at[r]).wait_send()
 
     @pl.when(has_right)
     def _():
+        for s in range(STREAMS):
+            for r in range(ROUNDS):
+                right_copy(r, s).wait_send()
         count_r.wait_send()
-        for r in range(ROUNDS):
-            to_right(out_right.at[r], in_left.at[r], send_r.at[r], recv_r.at[r]).wait_send()
-        pltpu.make_async_copy(slot_in, slot_in, slot_sem.at[0]).wait()
-
-    for r in range(ROUNDS):
-        taken(first_in if r == 0 else c_in.at[r - 1], c_send.at[r])
+        pltpu.make_async_copy(slot0_in, slot0_in, slot_sem.at[0, 0]).wait()
+        for r in range(2, ROUNDS):
+            pltpu.make_async_copy(slot_in.at[r - 2], slot_in.at[r - 2], slot_sem.at[r - 1, 0]).wait()
+
+    taken(c0_in, c_sem.at[0, 0])
+    for r in range(2, ROUNDS):
+        taken(c_in.at[r - 2], c_sem.at[r - 1, 0])
 
 
 def finish(theta, gen, base, theta_o, gen_o, base_o, sem):
-    copies = [
-        pltpu.make_async_copy(src, dst, sem.at[i])
-        for i, (src, dst) in enumerate([(theta, theta_o), (gen, gen_o), (base, base_o)])
-    ]
+    copies = [pltpu.make_async_copy(base, base_o, sem.at[0])]
+    rows = theta.shape[0] // CHUNKS
+    for i in range(CHUNKS):
+        part = pl.ds(i * rows, rows)
+        copies.append(pltpu.make_async_copy(theta.at[part], theta_o.at[part], sem.at[1 + i]))
+        copies.append(pltpu.make_async_copy(gen.at[part], gen_o.at[part], sem.at[1 + CHUNKS + i]))
     for copy in copies:
         copy.start()
     for copy in copies:
@@ -544,31 +581,32 @@
             vmem((2 * slots, branches), BF16),
             vmem((2 * slots, branches), BF16),
             vmem((slots, buses), BF16),
-            vmem((conts, slots), F32),
-            vmem((conts, slots), F32),
+            vmem((STREAMS, conts // STREAMS, slots), F32),
+            vmem((STREAMS, conts // STREAMS, slots), F32),
             vmem((2, 8, slots), F32),
             vmem((2, 8, slots), F32),
-            vmem((ROUNDS, conts, slots), F32),
-            vmem((ROUNDS, conts, slots), F32),
-            vmem((ROUNDS, conts, slots), F32),
-            vmem((ROUNDS, conts, slots), F32),
-            vmem((2 * blocks, LANES), F32),
-            vmem((n_cont, 2 * blocks, LANES), F32),
-            vmem((ROUNDS - 1, blocks, LANES), F32),
-            vmem((ROUNDS - 1, n_cont, blocks, LANES), F32),
-            vmem((1, slots), F32),
-            vmem((n_cont, 1, slots), F32),
+            vmem((ROUNDS, STREAMS, conts // STREAMS, slots), F32),
+            vmem((ROUNDS, STREAMS, conts // STREAMS, slots), F32),
+            vmem((ROUNDS, STREAMS, conts // STREAMS, slots), F32),
+            vmem((ROUNDS, STREAMS, conts // STREAMS, slots), F32),
+            vmem((3, blocks, LANES), F32),
+            vmem((n_cont, 3, blocks, LANES), F32),
+            vmem((2, blocks, LANES), F32),
+            vmem((2, n_cont, blocks, LANES), F32),
+            vmem((2, slots), F32),
+            vmem((n_cont, 2, slots), F32),
+            vmem((2, 1, slots), F32),
+            vmem((2, n_cont, 1, slots), F32),
             dma((13,)),
+            dma((2, STREAMS)),
             dma((2,)),
             dma((2,)),
-            dma((2,)),
-            dma((ROUNDS,)),
-            dma((ROUNDS,)),
-            dma((ROUNDS,)),
-            dma((ROUNDS,)),
-            dma((ROUNDS,)),
-            dma((ROUNDS,)),
-            dma((2,)),
+            dma((ROUNDS, STREAMS)),
+            dma((ROUNDS, STREAMS)),
+            dma((ROUNDS, STREAMS)),
+            dma((ROUNDS, STREAMS)),
+            dma((3, 2)),
+            dma((3, 2)),
             pltpu.SemaphoreType.REGULAR,
             pltpu.SemaphoreType.REGULAR,
         ],
@@ -600,7 +638,7 @@
         ),
         in_specs=[inside] * 3,
         out_specs=(outside,) * 3,
-        scratch_shapes=[dma((3,))],
+        scratch_shapes=[dma((1 + 2 * CHUNKS,))],
         compiler_params=pltpu.CompilerParams(vmem_limit_bytes=4 << 20),
         name="finish",
     )(*kept)

time: 27 us -> 26.3 us (0.974)
  Pallas kernels: 26.2 us -> 25.5 us
    pallas_call x1, Pallas kernels: 25.5 us -> 24.8 us  [local(): pl.pallas_call(functools.partial(kernel, n_cont, n_net, row), out_shape=(...]
where the time goes in v3:
time: 26.3 us; the launch traced here: 26.2 us
  Pallas kernels  25.5 us (97%)
  between operations  0.64 us (2%)
    pallas_call x1, Pallas kernels, local(): pl.pallas_call(functools.partial(kernel, n_cont, n_net, row), out_shape=(...  24.8 us
    pallas_call x1, Pallas kernels, local(): pl.pallas_call(finish, out_shape=(jax.ShapeDtypeStruct((conts, buses), F3...  0.77 us

profile of v3, /device:TPU:384, one launch (start us, length us, event | category | flops | bytes accessed | tf_op | source)
XLA Modules:
  0.0 26.2 jit_solution(1842955174350689404)
XLA Ops:
  0.6 24.8 %rounds.1 = (f32[64,512]{1,0:T(8,128)S(1)}, f32[64,512]{1,0:T(8,128)S(1)}, f32[4,128]{1,0:T(4,128)S(1)}) custom-call(f32[64,512]{1,0:T(8,128)} %angles_h.1, f32[64,640]{1,0:T(8,128)} %lam_f_h.1, f32[64,640]{1,0:T(8,128)} %lam_t_h.1, f32[64,512]{1,0:T(8,128)} %dual_h.1, s32[64,640]{1,0:T(8,128)} %outage_h.1, s32[5,128]{1,0:T(8,128)} %bitcast.9, ...), custom_call_target="tpu_custom_call" | custom-call | tf_op jit(solution)/shard_map/rounds/pallas_call | solution.py:556
  25.4 0.8 %finish.1 = (f32[64,512]{1,0:T(8,128)}, f32[64,512]{1,0:T(8,128)}, f32[4,128]{1,0:T(4,128)}) custom-call(f32[64,512]{1,0:T(8,128)S(1)} %get-tuple-element.9.theta, f32[64,512]{1,0:T(8,128)S(1)} %get-tuple-element.10.gen, f32[4,128]{1,0:T(4,128)S(1)} %get-tuple-element.11.base), custom_call_target="tpu_custom_call" | custom-call | tf_op jit(solution)/shard_map/finish/pallas_call | solution.py:632

commit v4 on v3

--- a/solution.py
+++ b/solution.py
@@ -10,7 +10,7 @@
 ROUNDS = 4
 LANES = 128
 STREAMS = 2
-CHUNKS = 4
+CHUNKS = 1
 penalty = 1.0
 balance = 2.0
 F32 = jnp.float32
@@ -97,6 +97,9 @@
     slot0_in,
     slot_out,
     slot_in,
+    zeros,
+    where_at,
+    if_any,
     in_sem,
     pick_sem,
     count_send,
@@ -147,19 +150,6 @@
         copy.start()
         loads.append(copy)
 
-    @pl.when(jnp.logical_not(has_left))
-    def _():
-        count_in[0] = jnp.zeros((8, slots), F32)
-        in_left[...] = jnp.zeros_like(in_left)
-        slot0_in[...] = jnp.zeros_like(slot0_in)
-        slot_in[...] = jnp.zeros_like(slot_in)
-
-    @pl.when(jnp.logical_not(has_right))
-    def _():
-        count_in[1] = jnp.zeros((8, slots), F32)
-        pick_in[...] = jnp.zeros_like(pick_in)
-        in_right[...] = jnp.zeros_like(in_right)
-
     barrier = pltpu.get_barrier_semaphore()
     column = [lax.rem(my_row + j, n_rows) * row + my_col for j in range(1, n_rows)]
     near = [my_row * row + lax.rem(my_col + j, row) for j in range(1, row)] + column
@@ -186,15 +176,12 @@
     loads[0].wait()
     rows = rows_v[...]
     rows = jnp.where(rows < buses, rows, -1)
-    rows_c = jnp.transpose(jnp.broadcast_to(rows.astype(F32), (slots, slots))).astype(jnp.int32)
-    lane = lax.broadcasted_iota(jnp.int32, (slots, LANES), 1)
-    slot_id = lax.broadcasted_iota(jnp.int32, (slots, LANES), 0)
-    for j in range(blocks):
-        listed[:, j * LANES : (j + 1) * LANES] = is_at(rows_c, lane + j * LANES).astype(BF16)
+    bus_id = lax.broadcasted_iota(jnp.int32, (buses, slots), 0)
+    listed[...] = is_at(bus_id, rows).astype(BF16)
     loads[1].wait()
     theta0 = theta[...]
     theta2 = pieces(theta0)
-    picked = times_t(theta2, listed[...])
+    picked = times(theta2, listed[...])
     for s in range(STREAMS):
         pick_out[s] = picked[s * part_rows : (s + 1) * part_rows]
 
@@ -228,9 +215,33 @@
         for s in range(STREAMS):
             pick(s).start()
 
+    def nothing(dst, sem):
+        pltpu.make_async_copy(zeros.at[pl.ds(0, dst.shape[0])], dst, sem).start()
+
+    zeros[...] = jnp.zeros_like(zeros)
+
+    @pl.when(jnp.logical_not(has_left))
+    def _():
+        slot0_in[...] = jnp.zeros_like(slot0_in)
+        slot_in[...] = jnp.zeros_like(slot_in)
+        nothing(count_in.at[0], count_recv.at[1])
+        for r in range(ROUNDS):
+            for s in range(STREAMS):
+                nothing(in_left.at[r, s], recv_r.at[r, s])
+
+    @pl.when(jnp.logical_not(has_right))
+    def _():
+        nothing(count_in.at[1], count_recv.at[0])
+        for s in range(STREAMS):
+            nothing(pick_in.at[s], pick_sem.at[1, s])
+            for r in range(ROUNDS - 1):
+                nothing(in_right.at[r, s], recv_l.at[r, s])
+
     for c in column:
         pl.semaphore_signal(plane_sem, inc=1, **at(c, part))
 
+    rows_c = jnp.transpose(jnp.broadcast_to(rows.astype(F32), (slots, slots))).astype(jnp.int32)
+    slot_id = lax.broadcasted_iota(jnp.int32, (slots, LANES), 0)
     loads[2].wait()
     loads[3].wait()
     for j in range(branches // LANES):
@@ -262,7 +273,36 @@
     def _():
         count_r.start()
 
-    bus_id = lax.broadcasted_iota(jnp.int32, (buses, LANES), 0)
+    kind = lax.broadcasted_iota(jnp.int32, (16, slots), 0)
+    probe = jnp.where(kind == 0, lax.broadcasted_iota(jnp.int32, (16, slots), 1), kind)
+    probe = jnp.where(kind < 2, probe, 0).astype(F32).astype(BF16)
+    differ = jnp.dot(probe, edge[:slots, :], preferred_element_type=F32)
+    both = jnp.dot(probe, edge_count[:slots, :], preferred_element_type=F32)
+    ends = [0.5 * (both + differ), 0.5 * (both - differ)]
+    for j in range(branches // LANES):
+        cols = slice(j * LANES, (j + 1) * LANES)
+        for k in range(2):
+            where_at[k, j] = jnp.broadcast_to(ends[k][0:1, cols], (8, LANES)).astype(jnp.int32)
+            if_any[k, j] = jnp.broadcast_to(ends[k][1:2, cols], (8, LANES))
+        beyond = jnp.broadcast_to(to_v[j : j + 1, :] - buses, (8, LANES))
+        where_at[2, j] = jnp.maximum(beyond, 0)
+        if_any[2, j] = jnp.where(beyond >= 0, 1.0, 0.0).astype(F32)
+
+    def reach(values, k, j):
+        times_8 = part_rows // 8
+        index = jnp.concatenate([where_at[k, j]] * times_8, axis=0)
+        mask = jnp.concatenate([if_any[k, j]] * times_8, axis=0)
+        return mask * jnp.take_along_axis(values, index, axis=1)
+
+    def reached(values, change=None):
+        out = []
+        for j in range(branches // LANES):
+            gap = -reach(values, 2, j)
+            if change is not None:
+                gap = gap + (reach(change, 0, j) - reach(change, 1, j))
+            out.append(gap)
+        return jnp.concatenate(out, axis=1)
+
     for j in range(branches // LANES):
         cols = slice(j * LANES, (j + 1) * LANES)
         a = is_at(bus_id, from_v[j : j + 1, :])
@@ -321,80 +361,79 @@
         for s in range(STREAMS):
             block = slice(s * part_rows, (s + 1) * part_rows)
 
-            @pl.when(has_right)
-            def _():
-                if r == 0:
-                    pick(s).wait_recv()
-                else:
-                    left_copy(r - 1, s).wait_recv()
-
+            if r == 0:
+                pick(s).wait_recv()
+            else:
+                left_copy(r - 1, s).wait_recv()
+                right_copy(r - 1, s).wait_recv()
             if r == 0:
                 halos[s] = pick_in[s]
-                added = times(pieces(halos[s]), edge[slots:, :])
+                added = reached(halos[s])
                 deltas.append(delta[block] + added)
                 flows.append(share[block] * (rest[block] + added))
             else:
-
-                @pl.when(has_left)
-                def _():
-                    right_copy(r - 1, s).wait_recv()
-
                 left = in_left[r - 1, s]
                 lefts.append(left)
                 halos[s] = keep_halo * halos[s] - (in_right[r - 1, s] + slot_nets[s]) * inv_halo
-                arrived = jnp.concatenate([-left * inv_listed, halos[s]], axis=1)
-                gap = rest[block] + 2.0 * times(pieces(arrived), edge[...])
+                gap = rest[block] + 2.0 * reached(halos[s], -left * inv_listed)
                 deltas.append(0.5 * (gap + delta[block]) - flow[block])
                 flows.append(share[block] * gap)
+            if last:
+                continue
             sent = times_t(pieces(flows[s]), edge[...])
             slot_nets[s] = sent[:, slots:]
             out_right[r, s] = slot_nets[s]
-            if not last:
-                out_left[r, s] = sent[:, :slots]
+            out_left[r, s] = sent[:, :slots]
 
             @pl.when(has_right)
             def _():
                 right_copy(r, s).start()
 
-            if not last:
-
-                @pl.when(has_left)
-                def _():
-                    left_copy(r, s).start()
+            @pl.when(has_left)
+            def _():
+                left_copy(r, s).start()
 
         flow = jnp.concatenate(flows, axis=0)
         delta = jnp.concatenate(deltas, axis=0)
-        slot_sum = sum(jnp.sum(v, axis=0, keepdims=True) for v in slot_nets)
+        flow2 = pieces(flow)
+        if last:
+            slot_net = times_t(flow2, edge[slots:, :])
+        else:
+            slot_net = jnp.concatenate(slot_nets, axis=0)
+        slot_sum = jnp.sum(slot_net, axis=0, keepdims=True)
         if r < 2:
             slot0_out[r : r + 1, :] = slot_sum
         else:
             slot_out[r - 2] = slot_sum
             onward(slot_out.at[r - 2], slot_in.at[r - 2], slot_sem.at[r - 1])
-        net_here = times_t(pieces(flow), own[...])
+        if last:
+            for s in range(STREAMS):
+                out_right[r, s] = slot_net[s * part_rows : (s + 1) * part_rows]
+
+            @pl.when(has_right)
+            def _():
+                for s in range(STREAMS):
+                    right_copy(r, s).start()
+
+        net_here = times_t(flow2, own[...])
         store_sums(c0_out.at[r] if r < 2 else c_out.at[r - 2], net_here)
         if r >= 2:
             across(c_out.at[r - 2], c_in.at[r - 2], c_sem.at[r - 1])
 
         if r == 0:
 
-            @pl.when(has_right)
-            def _():
-                count_l.wait_recv()
-
-            @pl.when(has_left)
-            def _():
-                count_r.wait_recv()
-
+            count_l.wait_recv()
+            count_r.wait_recv()
             left_count = count_in[0]
             inv_halo = 1.0 / (count_in[1][:1] + slot_count[:1] + 1.0)
             keep_halo = 1.0 - inv_halo
             inv_listed = 1.0 / (listed_count[:1] + left_count[:1] + 1.0)
             left_count = jnp.concatenate([left_count, left_count], axis=0)
-            degree = own_count + times(pieces(left_count), listed[...])[:1]
+            degree = own_count + times_t(pieces(left_count), listed[...])[:1]
             inv_degree = 1.0 / (degree + 1.0)
             keep = 1.0 - inv_degree
         else:
-            spread = times(pieces(jnp.concatenate(lefts, axis=0)), listed[...])
+            spread = times_t(pieces(jnp.concatenate(lefts, axis=0)), listed[...])
             net = net + spread
             now = now - spread * inv_degree
             dual_part = dual_part - (dual_part - 2.0 * net) * inv_row
@@ -432,7 +471,7 @@
         tall = jnp.concatenate(
             [slot_sums, jnp.zeros((16 - slot_sums.shape[0], slots), F32)], axis=0
         )
-        wide = times(pieces(tall), listed[...])
+        wide = times_t(pieces(tall), listed[...])
         return [
             jnp.concatenate([wide[r : r + 1, j * LANES : (j + 1) * LANES] for j in range(blocks)], axis=0)
             for r in range(slot_sums.shape[0])
@@ -458,13 +497,9 @@
 
     lefts = []
     for s in range(STREAMS):
-
-        @pl.when(has_left)
-        def _():
-            right_copy(ROUNDS - 1, s).wait_recv()
-
+        right_copy(ROUNDS - 1, s).wait_recv()
         lefts.append(in_left[ROUNDS - 1, s])
-    spread = times(pieces(jnp.concatenate(lefts, axis=0)), listed[...])
+    spread = times_t(pieces(jnp.concatenate(lefts, axis=0)), listed[...])
     theta_o[...] = now - spread * inv_degree
     net = net + spread
     part_gen = (balance * net - dual_part) * inv_row
@@ -580,7 +615,7 @@
             vmem((buses, branches), BF16),
             vmem((2 * slots, branches), BF16),
             vmem((2 * slots, branches), BF16),
-            vmem((slots, buses), BF16),
+            vmem((buses, slots), BF16),
             vmem((STREAMS, conts // STREAMS, slots), F32),
             vmem((STREAMS, conts // STREAMS, slots), F32),
             vmem((2, 8, slots), F32),
@@ -597,6 +632,9 @@
             vmem((n_cont, 2, slots), F32),
             vmem((2, 1, slots), F32),
             vmem((2, n_cont, 1, slots), F32),
+            vmem((conts, slots), F32),
+            vmem((3, branches // LANES, 8, LANES), i32),
+            vmem((3, branches // LANES, 8, LANES), F32),
             dma((13,)),
             dma((2, STREAMS)),
             dma((2,)),

time: 26.3 us -> 26 us (0.989)
  Pallas kernels: 25.5 us -> 25.2 us
    pallas_call x1, Pallas kernels: 24.8 us -> 24.5 us  [local(): pl.pallas_call(functools.partial(kernel, n_cont, n_net, row), out_shape=(...]
where the time goes in v4:
time: 26 us; the launch traced here: 25.9 us
  Pallas kernels  25.2 us (97%)
  between operations  0.64 us (2%)
    pallas_call x1, Pallas kernels, local(): pl.pallas_call(functools.partial(kernel, n_cont, n_net, row), out_shape=(...  24.5 us
    pallas_call x1, Pallas kernels, local(): pl.pallas_call(finish, out_shape=(jax.ShapeDtypeStruct((conts, buses), F3...  0.73 us

profile of v4, /device:TPU:384, one launch (start us, length us, event | category | flops | bytes accessed | tf_op | source)
XLA Modules:
  0.0 25.9 jit_solution(3941845243170388850)
XLA Ops:
  0.6 24.5 %rounds.1 = (f32[64,512]{1,0:T(8,128)S(1)}, f32[64,512]{1,0:T(8,128)S(1)}, f32[4,128]{1,0:T(4,128)S(1)}) custom-call(f32[64,512]{1,0:T(8,128)} %angles_h.1, f32[64,640]{1,0:T(8,128)} %lam_f_h.1, f32[64,640]{1,0:T(8,128)} %lam_t_h.1, f32[64,512]{1,0:T(8,128)} %dual_h.1, s32[64,640]{1,0:T(8,128)} %outage_h.1, s32[5,128]{1,0:T(8,128)} %bitcast.9, ...), custom_call_target="tpu_custom_call" | custom-call | tf_op jit(solution)/shard_map/rounds/pallas_call | solution.py:591
  25.1 0.7 %finish.1 = (f32[64,512]{1,0:T(8,128)}, f32[64,512]{1,0:T(8,128)}, f32[4,128]{1,0:T(4,128)}) custom-call(f32[64,512]{1,0:T(8,128)S(1)} %get-tuple-element.9.theta, f32[64,512]{1,0:T(8,128)S(1)} %get-tuple-element.10.gen, f32[4,128]{1,0:T(4,128)S(1)} %get-tuple-element.11.base), custom_call_target="tpu_custom_call" | custom-call | tf_op jit(solution)/shard_map/finish/pallas_call | solution.py:670

commit v5 on v4

--- a/solution.py
+++ b/solution.py
@@ -64,18 +64,13 @@
     gen_o,
     base_o,
     theta,
-    lam_f,
-    lam_t,
+    lam,
     dual,
     outage,
-    from_v,
-    to_v,
+    ends_v,
     rows_v,
     stiff,
-    base_v,
-    load,
-    cost,
-    limit,
+    params,
     own,
     count,
     edge,
@@ -87,8 +82,9 @@
     count_in,
     out_left,
     out_right,
-    in_left,
-    in_right,
+    inbox,
+    last_out,
+    last_in,
     c0_out,
     c0_in,
     c_out,
@@ -100,21 +96,18 @@
     zeros,
     where_at,
     if_any,
+    sem,
+    pick_sem,
+    count_sem,
     in_sem,
-    pick_sem,
-    count_send,
-    count_recv,
-    send_l,
-    recv_l,
-    send_r,
-    recv_r,
+    last_sem,
     c_sem,
     slot_sem,
     plane_sem,
     next_sem,
 ):
     conts, buses = theta.shape
-    branches = lam_f.shape[1]
+    branches = outage.shape[1]
     slots = rows_v.shape[1]
     blocks = buses // LANES
     part_rows = conts // STREAMS
@@ -128,27 +121,25 @@
     def at(c, p):
         return dict(device_id={"cont": c, "net": p}, device_id_type=MESH)
 
-    loads = []
-    for i, (src, dst) in enumerate(
-        [
-            (rows_h, rows_v),
-            (angles_h, theta),
-            (from_h, from_v),
-            (to_h, to_v),
-            (lam_f_h, lam_f),
-            (lam_t_h, lam_t),
-            (outage_h, outage),
-            (stiff_h, stiff),
-            (dual_h, dual),
-            (base_h, base_v),
-            (load_h, load),
-            (cost_h, cost),
-            (limit_h, limit),
-        ]
-    ):
-        copy = pltpu.make_async_copy(src, dst, in_sem.at[i])
-        copy.start()
-        loads.append(copy)
+    for src, dst, i in [
+        (rows_h, rows_v, 0),
+        (angles_h, theta, 1),
+        (from_h, ends_v.at[0], 2),
+        (to_h, ends_v.at[1], 2),
+        (lam_f_h, lam.at[0], 3),
+        (lam_t_h, lam.at[1], 3),
+        (outage_h, outage, 4),
+        (stiff_h, stiff, 5),
+        (dual_h, dual, 6),
+        (base_h, params.at[0], 7),
+        (load_h, params.at[1], 7),
+        (cost_h, params.at[2], 7),
+        (limit_h, params.at[3], 7),
+    ]:
+        pltpu.make_async_copy(src, dst, sem.at[i]).start()
+
+    def loaded(ref, i):
+        pltpu.make_async_copy(ref, ref, sem.at[i]).wait()
 
     barrier = pltpu.get_barrier_semaphore()
     column = [lax.rem(my_row + j, n_rows) * row + my_col for j in range(1, n_rows)]
@@ -173,12 +164,12 @@
         lax.rem(my_row + i, n_rows) * row + lax.rem(my_col + j, row) for i, j in steps
     ]
 
-    loads[0].wait()
+    loaded(rows_v, 0)
     rows = rows_v[...]
     rows = jnp.where(rows < buses, rows, -1)
     bus_id = lax.broadcasted_iota(jnp.int32, (buses, slots), 0)
     listed[...] = is_at(bus_id, rows).astype(BF16)
-    loads[1].wait()
+    loaded(theta, 1)
     theta0 = theta[...]
     theta2 = pieces(theta0)
     picked = times(theta2, listed[...])
@@ -202,13 +193,17 @@
         return pltpu.make_async_remote_copy(src, dst, s, r, **at(me, part + 1))
 
     def pick(s):
-        return to_left(pick_out.at[s], pick_in.at[s], pick_sem.at[0, s], pick_sem.at[1, s])
+        return to_left(pick_out.at[s], pick_in.at[s], sem.at[s], pick_sem.at[s])
 
     def left_copy(r, s):
-        return to_left(out_left.at[r, s], in_right.at[r, s], send_l.at[r, s], recv_l.at[r, s])
+        return to_left(out_left.at[r, s], inbox.at[r, s, 1], sem.at[3 + s], in_sem.at[r, s])
 
     def right_copy(r, s):
-        return to_right(out_right.at[r, s], in_left.at[r, s], send_r.at[r, s], recv_r.at[r, s])
+        return to_right(out_right.at[r, s], inbox.at[r, s, 0], sem.at[3 + STREAMS + s], in_sem.at[r, s])
+
+    last_copy = to_right(last_out, last_in, sem.at[3], last_sem)
+    local_send = sem.at[3 + 2 * STREAMS]
+    slot_send = sem.at[4 + 2 * STREAMS]
 
     @pl.when(has_left)
     def _():
@@ -224,26 +219,27 @@
     def _():
         slot0_in[...] = jnp.zeros_like(slot0_in)
         slot_in[...] = jnp.zeros_like(slot_in)
-        nothing(count_in.at[0], count_recv.at[1])
-        for r in range(ROUNDS):
+        nothing(count_in.at[0], count_sem)
+        nothing(last_in, last_sem)
+        for r in range(ROUNDS - 1):
             for s in range(STREAMS):
-                nothing(in_left.at[r, s], recv_r.at[r, s])
+                nothing(inbox.at[r, s, 0], in_sem.at[r, s])
 
     @pl.when(jnp.logical_not(has_right))
     def _():
-        nothing(count_in.at[1], count_recv.at[0])
+        nothing(count_in.at[1], count_sem)
         for s in range(STREAMS):
-            nothing(pick_in.at[s], pick_sem.at[1, s])
+            nothing(pick_in.at[s], pick_sem.at[s])
             for r in range(ROUNDS - 1):
-                nothing(in_right.at[r, s], recv_l.at[r, s])
+                nothing(inbox.at[r, s, 1], in_sem.at[r, s])
 
     for c in column:
         pl.semaphore_signal(plane_sem, inc=1, **at(c, part))
 
     rows_c = jnp.transpose(jnp.broadcast_to(rows.astype(F32), (slots, slots))).astype(jnp.int32)
     slot_id = lax.broadcasted_iota(jnp.int32, (slots, LANES), 0)
-    loads[2].wait()
-    loads[3].wait()
+    loaded(ends_v, 2)
+    from_v, to_v = ends_v.at[0], ends_v.at[1]
     for j in range(branches // LANES):
         cols = slice(j * LANES, (j + 1) * LANES)
         start = from_v[j : j + 1, :]
@@ -262,8 +258,8 @@
     listed_count, slot_count = counts[:8, :slots], counts[:8, slots:]
     count_out[0] = listed_count
     count_out[1] = slot_count
-    count_l = to_left(count_out.at[0], count_in.at[1], count_send.at[0], count_recv.at[0])
-    count_r = to_right(count_out.at[1], count_in.at[0], count_send.at[1], count_recv.at[1])
+    count_l = to_left(count_out.at[0], count_in.at[1], sem.at[2], count_sem)
+    count_r = to_right(count_out.at[1], count_in.at[0], slot_send, count_sem)
 
     @pl.when(has_left)
     def _():
@@ -279,6 +275,16 @@
     differ = jnp.dot(probe, edge[:slots, :], preferred_element_type=F32)
     both = jnp.dot(probe, edge_count[:slots, :], preferred_element_type=F32)
     ends = [0.5 * (both + differ), 0.5 * (both - differ)]
+    of_bus = lax.dot_general(
+        probe, listed[...], (((1,), (1,)), ((), ())), preferred_element_type=F32
+    )
+    fill = [jnp.zeros((8 - blocks, LANES), F32)]
+
+    def in_blocks(v):
+        return jnp.concatenate([v[:, j * LANES : (j + 1) * LANES] for j in range(blocks)] + fill, axis=0)
+
+    bus_slot = in_blocks(of_bus[0:1]).astype(jnp.int32)
+    bus_listed = in_blocks(of_bus[1:2])
     for j in range(branches // LANES):
         cols = slice(j * LANES, (j + 1) * LANES)
         for k in range(2):
@@ -308,11 +314,10 @@
         a = is_at(bus_id, from_v[j : j + 1, :])
         b = is_at(bus_id, to_v[j : j + 1, :])
         own[:, cols] = (a - b).astype(BF16)
-        count[:, cols] = (a + b).astype(BF16)
     delta = times(theta2, own[...])
 
-    for copy in loads[4:]:
-        copy.wait()
+    for ref, i in [(lam, 3), (outage, 4), (stiff, 5), (dual, 6), (params, 7)]:
+        loaded(ref, i)
     share = []
     for j in range(branches // LANES):
         cols = slice(j * LANES, (j + 1) * LANES)
@@ -320,12 +325,9 @@
         full = full / (penalty + 2.0 * full)
         share.append(full * (1.0 - outage[:, cols].astype(F32)))
     share = jnp.concatenate(share, axis=1)
-    rest = delta - (lam_f[...] - lam_t[...])
-
-    own_count = lax.dot_general(
-        ones, count[...], (((1,), (1,)), ((), ())), preferred_element_type=F32
-    )[:1]
-    inv_cost = 1.0 / (cost[...] + (penalty + balance))
+    rest = delta - (lam[0] - lam[1])
+
+    inv_cost = 1.0 / (params[2] + (penalty + balance))
     dual_part = dual[...]
     inv_row = jnp.concatenate([inv_cost[j : j + 1, :] for j in range(blocks)], axis=1)
 
@@ -336,20 +338,29 @@
 
     store_sums(c0_out.at[2], dual_part)
 
-    def across(src, dst, sem):
+    def across(src, dst, arrived):
         dst[me] = src[...]
         for c in plane[:-1]:
             pltpu.make_async_remote_copy(
-                src, dst.at[me], sem.at[0], sem.at[1], **at(c, part)
+                src, dst.at[me], local_send, arrived, **at(c, part)
             ).start()
 
-    def onward(src, dst, sem):
+    def onward(src, dst, arrived):
         @pl.when(has_right)
         def _():
             for c in plane:
                 pltpu.make_async_remote_copy(
-                    src, dst.at[me], sem.at[0], sem.at[1], **at(c, part + 1)
+                    src, dst.at[me], slot_send, arrived, **at(c, part + 1)
                 ).start()
+
+    def taken(ref, arrived):
+        some = ref.at[pl.ds(0, n_cont - 1)]
+        pltpu.make_async_copy(some, some, arrived).wait()
+
+    def onward_sent(ref):
+        @pl.when(has_right)
+        def _():
+            pltpu.make_async_copy(ref, ref, slot_send).wait()
 
     halos = [None] * STREAMS
     slot_nets = [None] * STREAMS
@@ -364,17 +375,17 @@
             if r == 0:
                 pick(s).wait_recv()
             else:
-                left_copy(r - 1, s).wait_recv()
-                right_copy(r - 1, s).wait_recv()
+                box = inbox.at[r - 1, s]
+                pltpu.make_async_copy(box, box, in_sem.at[r - 1, s]).wait()
             if r == 0:
                 halos[s] = pick_in[s]
                 added = reached(halos[s])
                 deltas.append(delta[block] + added)
                 flows.append(share[block] * (rest[block] + added))
             else:
-                left = in_left[r - 1, s]
+                left = inbox[r - 1, s, 0]
                 lefts.append(left)
-                halos[s] = keep_halo * halos[s] - (in_right[r - 1, s] + slot_nets[s]) * inv_halo
+                halos[s] = keep_halo * halos[s] - (inbox[r - 1, s, 1] + slot_nets[s]) * inv_halo
                 gap = rest[block] + 2.0 * reached(halos[s], -left * inv_listed)
                 deltas.append(0.5 * (gap + delta[block]) - flow[block])
                 flows.append(share[block] * gap)
@@ -397,33 +408,59 @@
         delta = jnp.concatenate(deltas, axis=0)
         flow2 = pieces(flow)
         if last:
-            slot_net = times_t(flow2, edge[slots:, :])
+            whole = jnp.broadcast_to(jnp.sum(flow, axis=0, keepdims=True), (16, branches))
+            whole2 = pieces(whole)
+            slot_sum = times_t(whole2, edge[slots:, :])[:1]
         else:
             slot_net = jnp.concatenate(slot_nets, axis=0)
-        slot_sum = jnp.sum(slot_net, axis=0, keepdims=True)
+            slot_sum = jnp.sum(slot_net, axis=0, keepdims=True)
         if r < 2:
             slot0_out[r : r + 1, :] = slot_sum
         else:
             slot_out[r - 2] = slot_sum
+            if not last:
+                onward_sent(slot0_in)
             onward(slot_out.at[r - 2], slot_in.at[r - 2], slot_sem.at[r - 1])
         if last:
-            for s in range(STREAMS):
-                out_right[r, s] = slot_net[s * part_rows : (s + 1) * part_rows]
+            store_sums(c_out.at[1], times_t(whole2, own[...])[:1])
+            across(c_out.at[1], c_in.at[1], c_sem.at[2])
+            slot_net = times_t(flow2, edge[slots:, :])
+            last_out[...] = slot_net
 
             @pl.when(has_right)
             def _():
+                last_copy.start()
+
+        net_here = times_t(flow2, own[...])
+        if r < 2:
+            store_sums(c0_out.at[r], net_here)
+        elif not last:
+            store_sums(c_out.at[0], net_here)
+            taken(c0_in, local_send)
+            across(c_out.at[0], c_in.at[0], c_sem.at[1])
+
+        if r == 0:
+
+            for j in range(branches // LANES):
+                cols = slice(j * LANES, (j + 1) * LANES)
+                a = is_at(bus_id, from_v[j : j + 1, :])
+                b = is_at(bus_id, to_v[j : j + 1, :])
+                count[:, cols] = (a + b).astype(BF16)
+            own_count = lax.dot_general(
+                ones, count[...], (((1,), (1,)), ((), ())), preferred_element_type=F32
+            )[:1]
+            pltpu.make_async_copy(count_in, count_in, count_sem).wait()
+
+            @pl.when(has_left)
+            def _():
                 for s in range(STREAMS):
-                    right_copy(r, s).start()
-
-        net_here = times_t(flow2, own[...])
-        store_sums(c0_out.at[r] if r < 2 else c_out.at[r - 2], net_here)
-        if r >= 2:
-            across(c_out.at[r - 2], c_in.at[r - 2], c_sem.at[r - 1])
-
-        if r == 0:
-
-            count_l.wait_recv()
-            count_r.wait_recv()
+                    pick(s).wait_send()
+                count_l.wait_send()
+
+            @pl.when(has_right)
+            def _():
+                count_r.wait_send()
+
             left_count = count_in[0]
             inv_halo = 1.0 / (count_in[1][:1] + slot_count[:1] + 1.0)
             keep_halo = 1.0 - inv_halo
@@ -442,6 +479,21 @@
         now = keep * now - net * inv_degree
         if not last:
             rest = 2.0 * times(pieces(now), own[...]) + (2.0 * flow - delta)
+        if not last:
+
+            @pl.when(has_left)
+            def _():
+                for s in range(STREAMS):
+                    left_copy(r, s).wait_send()
+
+            @pl.when(has_right)
+            def _():
+                for s in range(STREAMS):
+                    right_copy(r, s).wait_send()
+
+        if r == 2:
+            taken(c_in.at[0], local_send)
+            onward_sent(slot_in.at[0])
         if r == 0:
             pl.semaphore_wait(plane_sem, len(column))
 
@@ -458,27 +510,17 @@
             onward(slot0_out, slot0_in, slot_sem.at[0])
             across(c0_out, c0_in, c_sem.at[0])
 
-    def taken(ref, sem):
-        some = ref.at[pl.ds(0, n_cont - 1)]
-        pltpu.make_async_copy(some, some, sem).wait()
-
-    def taken_here(ref, sem):
+    def taken_here(ref, arrived):
         @pl.when(has_left)
         def _():
-            pltpu.make_async_copy(ref, ref, sem).wait()
+            pltpu.make_async_copy(ref, ref, arrived).wait()
 
     def by_bus(slot_sums):
-        tall = jnp.concatenate(
-            [slot_sums, jnp.zeros((16 - slot_sums.shape[0], slots), F32)], axis=0
-        )
-        wide = times_t(pieces(tall), listed[...])
-        return [
-            jnp.concatenate([wide[r : r + 1, j * LANES : (j + 1) * LANES] for j in range(blocks)], axis=0)
-            for r in range(slot_sums.shape[0])
-        ]
-
-    loads_now = load[...]
-    limits = limit[...]
+        tall = jnp.broadcast_to(slot_sums, (8, slots))
+        return (bus_listed * jnp.take_along_axis(tall, bus_slot, axis=1))[:blocks]
+
+    loads_now = params[1]
+    limits = params[3]
     scale = 1.0 / (n_cont * conts)
 
     def update(x, mean_dual, beta, total):
@@ -487,22 +529,23 @@
         beta = beta + (x + balance * loads_now - beta) * inv_cost - x
         return jnp.clip(mean_gen + mean_dual, 0.0, limits), mean_dual, beta
 
-    taken(c0_in, c_sem.at[0, 1])
-    taken_here(slot0_in, slot_sem.at[0, 1])
+    taken(c0_in, c_sem.at[0])
+    taken_here(slot0_in, slot_sem.at[0])
     total = jnp.sum(c0_in[...], axis=0)
-    moved = by_bus(jnp.sum(slot0_in[...], axis=0))
-    state = (base_v[...], total[2] * scale, jnp.zeros_like(loads_now))
+    moved = jnp.sum(slot0_in[...], axis=0)
+    state = (params[0], total[2] * scale, jnp.zeros_like(loads_now))
     for r in range(2):
-        state = update(*state, total[r] + moved[r])
-
-    lefts = []
-    for s in range(STREAMS):
-        right_copy(ROUNDS - 1, s).wait_recv()
-        lefts.append(in_left[ROUNDS - 1, s])
-    spread = times_t(pieces(jnp.concatenate(lefts, axis=0)), listed[...])
+        state = update(*state, total[r] + by_bus(moved[r : r + 1]))
+
+    last_copy.wait_recv()
+    spread = times_t(pieces(last_in[...]), listed[...])
     theta_o[...] = now - spread * inv_degree
     net = net + spread
     part_gen = (balance * net - dual_part) * inv_row
+
+    @pl.when(has_right)
+    def _():
+        last_copy.wait_send()
 
     for r in range(2, ROUNDS):
         if r == ROUNDS - 1:
@@ -511,34 +554,14 @@
             for j in range(blocks):
                 cols = slice(j * LANES, (j + 1) * LANES)
                 gen_o[:, cols] = part_gen[:, cols] + row_gen[j : j + 1, :]
-        taken(c_in.at[r - 2], c_sem.at[r - 1, 1])
-        taken_here(slot_in.at[r - 2], slot_sem.at[r - 1, 1])
+        taken(c_in.at[r - 2], c_sem.at[r - 1])
+        taken_here(slot_in.at[r - 2], slot_sem.at[r - 1])
         total = jnp.sum(c_in[r - 2], axis=0)
-        moved = by_bus(jnp.sum(slot_in[r - 2], axis=0))
-        state = update(*state, total + moved[0])
+        state = update(*state, total + by_bus(jnp.sum(slot_in[r - 2], axis=0)))
     base_o[...] = state[0]
 
-    @pl.when(has_left)
-    def _():
-        for s in range(STREAMS):
-            pick(s).wait_send()
-            for r in range(ROUNDS - 1):
-                left_copy(r, s).wait_send()
-        count_l.wait_send()
-
-    @pl.when(has_right)
-    def _():
-        for s in range(STREAMS):
-            for r in range(ROUNDS):
-                right_copy(r, s).wait_send()
-        count_r.wait_send()
-        pltpu.make_async_copy(slot0_in, slot0_in, slot_sem.at[0, 0]).wait()
-        for r in range(2, ROUNDS):
-            pltpu.make_async_copy(slot_in.at[r - 2], slot_in.at[r - 2], slot_sem.at[r - 1, 0]).wait()
-
-    taken(c0_in, c_sem.at[0, 0])
-    for r in range(2, ROUNDS):
-        taken(c_in.at[r - 2], c_sem.at[r - 1, 0])
+    onward_sent(slot_in.at[1])
+    taken(c_in.at[1], local_send)
 
 
 def finish(theta, gen, base, theta_o, gen_o, base_o, sem):
@@ -599,18 +622,13 @@
         out_specs=(inside,) * 3,
         scratch_shapes=[
             vmem((conts, buses), F32),
-            vmem((conts, branches), F32),
-            vmem((conts, branches), F32),
+            vmem((2, conts, branches), F32),
             vmem((conts, buses), F32),
             vmem((conts, branches), i32),
-            vmem((branches // LANES, LANES), i32),
-            vmem((branches // LANES, LANES), i32),
+            vmem((2, branches // LANES, LANES), i32),
             vmem((1, slots), i32),
             vmem((branches // LANES, LANES), F32),
-            vmem((blocks, LANES), F32),
-            vmem((blocks, LANES), F32),
-            vmem((blocks, LANES), F32),
-            vmem((blocks, LANES), F32),
+            vmem((4, blocks, LANES), F32),
             vmem((buses, branches), BF16),
             vmem((buses, branches), BF16),
             vmem((2 * slots, branches), BF16),
@@ -620,10 +638,11 @@
             vmem((STREAMS, conts // STREAMS, slots), F32),
             vmem((2, 8, slots), F32),
             vmem((2, 8, slots), F32),
-            vmem((ROUNDS, STREAMS, conts // STREAMS, slots), F32),
-            vmem((ROUNDS, STREAMS, conts // STREAMS, slots), F32),
-            vmem((ROUNDS, STREAMS, conts // STREAMS, slots), F32),
-            vmem((ROUNDS, STREAMS, conts // STREAMS, slots), F32),
+            vmem((ROUNDS - 1, STREAMS, conts // STREAMS, slots), F32),
+            vmem((ROUNDS - 1, STREAMS, conts // STREAMS, slots), F32),
+            vmem((ROUNDS - 1, STREAMS, 2, conts // STREAMS, slots), F32),
+            vmem((conts, slots), F32),
+            vmem((conts, slots), F32),
             vmem((3, blocks, LANES), F32),
             vmem((n_cont, 3, blocks, LANES), F32),
             vmem((2, blocks, LANES), F32),
@@ -635,16 +654,13 @@
             vmem((conts, slots), F32),
             vmem((3, branches // LANES, 8, LANES), i32),
             vmem((3, branches // LANES, 8, LANES), F32),
-            dma((13,)),
-            dma((2, STREAMS)),
-            dma((2,)),
-            dma((2,)),
-            dma((ROUNDS, STREAMS)),
-            dma((ROUNDS, STREAMS)),
-            dma((ROUNDS, STREAMS)),
-            dma((ROUNDS, STREAMS)),
-            dma((3, 2)),
-            dma((3, 2)),
+            dma((5 + 2 * STREAMS,)),
+            dma((STREAMS,)),
+            dma,
+            dma((ROUNDS - 1, STREAMS)),
+            dma,
+            dma((3,)),
+            dma((3,)),
             pltpu.SemaphoreType.REGULAR,
             pltpu.SemaphoreType.REGULAR,
         ],

time: 26 us -> 25.4 us (0.977)
  Pallas kernels: 25.2 us -> 24.6 us
    pallas_call x1, Pallas kernels: 24.5 us -> 23.9 us  [local(): pl.pallas_call(functools.partial(kernel, n_cont, n_net, row), out_shape=(...]
where the time goes in v5:
time: 25.4 us; the launch traced here: 25.3 us
  Pallas kernels  24.6 us (97%)
  between operations  0.64 us (3%)
    pallas_call x1, Pallas kernels, local(): pl.pallas_call(functools.partial(kernel, n_cont, n_net, row), out_shape=(...  23.9 us
    pallas_call x1, Pallas kernels, local(): pl.pallas_call(finish, out_shape=(jax.ShapeDtypeStruct((conts, buses), F3...  0.73 us

profile of v5, /device:TPU:384, one launch (start us, length us, event | category | flops | bytes accessed | tf_op | source)
XLA Modules:
  0.0 25.3 jit_solution(18216739787082132830)
XLA Ops:
  0.6 23.9 %rounds.1 = (f32[64,512]{1,0:T(8,128)S(1)}, f32[64,512]{1,0:T(8,128)S(1)}, f32[4,128]{1,0:T(4,128)S(1)}) custom-call(f32[64,512]{1,0:T(8,128)} %angles_h.1, f32[64,640]{1,0:T(8,128)} %lam_f_h.1, f32[64,640]{1,0:T(8,128)} %lam_t_h.1, f32[64,512]{1,0:T(8,128)} %dual_h.1, s32[64,640]{1,0:T(8,128)} %outage_h.1, s32[5,128]{1,0:T(8,128)} %bitcast.9, ...), custom_call_target="tpu_custom_call" | custom-call | tf_op jit(solution)/shard_map/rounds/pallas_call | solution.py:614
  24.6 0.7 %finish.1 = (f32[64,512]{1,0:T(8,128)}, f32[64,512]{1,0:T(8,128)}, f32[4,128]{1,0:T(4,128)}) custom-call(f32[64,512]{1,0:T(8,128)S(1)} %get-tuple-element.9.theta, f32[64,512]{1,0:T(8,128)S(1)} %get-tuple-element.10.gen, f32[4,128]{1,0:T(4,128)S(1)} %get-tuple-element.11.base), custom_call_target="tpu_custom_call" | custom-call | tf_op jit(solution)/shard_map/finish/pallas_call | solution.py:686

commit v6 on v5

--- a/solution.py
+++ b/solution.py
@@ -414,6 +414,9 @@
         else:
             slot_net = jnp.concatenate(slot_nets, axis=0)
             slot_sum = jnp.sum(slot_net, axis=0, keepdims=True)
+        if last:
+            store_sums(c_out.at[1], times_t(whole2, own[...])[:1])
+            across(c_out.at[1], c_in.at[1], c_sem.at[2])
         if r < 2:
             slot0_out[r : r + 1, :] = slot_sum
         else:
@@ -422,8 +425,6 @@
                 onward_sent(slot0_in)
             onward(slot_out.at[r - 2], slot_in.at[r - 2], slot_sem.at[r - 1])
         if last:
-            store_sums(c_out.at[1], times_t(whole2, own[...])[:1])
-            across(c_out.at[1], c_in.at[1], c_sem.at[2])
             slot_net = times_t(flow2, edge[slots:, :])
             last_out[...] = slot_net
 

time: 25.4 us -> 25.5 us (level); the launches traced: 25.3 us -> 25.1 us
  no operation moved by 1% of the time
where the time goes in v6:
time: 25.5 us; the launch traced here: 25.1 us
  Pallas kernels  24.5 us (96%)
  between operations  0.64 us (3%)
    pallas_call x1, Pallas kernels, local(): pl.pallas_call(functools.partial(kernel, n_cont, n_net, row), out_shape=(...  23.7 us
    pallas_call x1, Pallas kernels, local(): pl.pallas_call(finish, out_shape=(jax.ShapeDtypeStruct((conts, buses), F3...  0.73 us

profile of v6, /device:TPU:384, one launch (start us, length us, event | category | flops | bytes accessed | tf_op | source)
XLA Modules:
  0.0 25.1 jit_solution(8617962143322147251)
XLA Ops:
  0.6 23.7 %rounds.1 = (f32[64,512]{1,0:T(8,128)S(1)}, f32[64,512]{1,0:T(8,128)S(1)}, f32[4,128]{1,0:T(4,128)S(1)}) custom-call(f32[64,512]{1,0:T(8,128)} %angles_h.1, f32[64,640]{1,0:T(8,128)} %lam_f_h.1, f32[64,640]{1,0:T(8,128)} %lam_t_h.1, f32[64,512]{1,0:T(8,128)} %dual_h.1, s32[64,640]{1,0:T(8,128)} %outage_h.1, s32[5,128]{1,0:T(8,128)} %bitcast.9, ...), custom_call_target="tpu_custom_call" | custom-call | tf_op jit(solution)/shard_map/rounds/pallas_call | solution.py:615
  24.4 0.7 %finish.1 = (f32[64,512]{1,0:T(8,128)}, f32[64,512]{1,0:T(8,128)}, f32[4,128]{1,0:T(4,128)}) custom-call(f32[64,512]{1,0:T(8,128)S(1)} %get-tuple-element.9.theta, f32[64,512]{1,0:T(8,128)S(1)} %get-tuple-element.10.gen, f32[4,128]{1,0:T(4,128)S(1)} %get-tuple-element.11.base), custom_call_target="tpu_custom_call" | custom-call | tf_op jit(solution)/shard_map/finish/pallas_call | solution.py:687
